TPU v7x, 256 devices: a whole 4x4x8 slice. The times are simulated.
256 devices in a mesh: pts: 32 (over z, y_hi, core), cam: 8 (over y_lo, x).
Axes of the slice: x: 4, y: 4 (y_hi: 2, y_lo: 2; y = y_hi * 2 + y_lo), z: 8, core: 2. Of those that a mesh axis runs over, the one named last changes fastest.
Arguments:
- rhs: float32 [8, 256, 576], P('cam', 'pts'), may hold values from -6 to 6
- damp_cam: float32 [8, 256, 576], P('cam', 'pts'), may hold values from 0.2 to 1
- precond: float32 [8, 256, 576], P('cam', 'pts'), may hold values from 0.3 to 3
- cam_jac: float32 [8, 3072, 8, 18, 128], P('cam', 'pts'), may hold values from -0.3125 to 0.3125
- pt_jac: float32 [8, 3072, 8, 6, 128], P('cam', 'pts'), may hold values from -6 to 6
- damp_pt: float32 [8, 3072, 3, 128], P('cam', 'pts'), may hold values from 0.5 to 8
- cam_index: int32 [8, 3072, 8, 128], P('cam', 'pts'), may hold values from 0 to 63
- tile_ids: int32 [8, 3072, 8], P('cam', 'pts'), may hold values from 0 to 511, as said below
- counts: int32 [8, 3072], P('cam', 'pts'), may hold values from 2 to 8, as said below
Outputs:
- solution: float32 [8, 256, 576], P('cam', 'pts')
- residual: float32 [8, 256, 576], P('cam', 'pts')
Inputs may be any that keep to these rules, and one draw needn't show every extreme that they name: `tile_ids`: point tile t of a group (t from 0 to 3071) lists only window tiles from (t * 256) // 3072 to that plus 256; entries at or beyond the tile's count are padding within the same range. `counts`: in every group the first point tile has all 8 entries live.
All inputs are finite; a program needn't handle non-finite values.
Results may differ from a plain program's by a relative error of at most 0.0003.
Values sent between devices are 32-bit elements; how exact they have to be, the bound alone decides.
A program may use at most 64 MiB of HBM per device.

v0:
```python
import math

import jax
import jax.numpy as jnp
from jax import lax
from jax.sharding import PartitionSpec as P

ITERS = 3


def from_behind(shard, axis, by):
    devices = lax.axis_size(axis)
    return lax.ppermute(shard, axis, [(i, (i + by) % devices) for i in range(devices)])


def point_inverse(pt_jac, counts, damp_pt):
    tiles = pt_jac.shape[0]
    slots = pt_jac.shape[1]
    points = pt_jac.shape[-1]
    live = (lax.iota(jnp.int32, slots)[None, :] < counts[:, None]).astype(jnp.float32)
    shaped = pt_jac.reshape(tiles, slots, 2, 3, points)
    gram = jnp.sum(
        live[:, :, None, None, None, None]
        * shaped[:, :, :, :, None, :]
        * shaped[:, :, :, None, :, :],
        axis=(1, 2),
    )
    gram = gram + damp_pt[:, :, None, :] * jnp.eye(3, dtype=jnp.float32)[None, :, :, None]
    first = jnp.roll(jnp.roll(gram, -1, axis=1), -1, axis=2)
    second = jnp.roll(jnp.roll(gram, -2, axis=1), -2, axis=2)
    mixed_one = jnp.roll(jnp.roll(gram, -1, axis=1), -2, axis=2)
    mixed_two = jnp.roll(jnp.roll(gram, -2, axis=1), -1, axis=2)
    cofactor = first * second - mixed_one * mixed_two
    determinant = jnp.sum(gram[:, 0] * cofactor[:, 0], axis=1)
    return cofactor / determinant[:, None, None, :]


def block_term(window, total, item):
    jac_cam, jac_point, index_cam, index_tile, live_block, inverse_block = item
    blocks, slots, points = index_cam.shape
    cameras = window.shape[1] // 9
    picked_tiles = jnp.take(window, index_tile, axis=0).reshape(blocks, slots, 9, cameras)
    selector = (
        index_cam[:, :, None, :] == lax.iota(jnp.int32, cameras)[None, None, :, None]
    ).astype(jnp.float32)
    picked = jnp.einsum("bsjc,bscp->bsjp", picked_tiles, selector, precision=lax.Precision.HIGHEST)
    cam_rows = jac_cam.reshape(blocks, slots, 2, 9, points)
    point_rows = jac_point.reshape(blocks, slots, 2, 3, points)
    masked = live_block[:, :, None, None]
    residual_rows = jnp.sum(cam_rows * picked[:, :, None], axis=3) * masked
    point_side = jnp.sum(point_rows * residual_rows[:, :, :, None, :], axis=(1, 2))
    solved = jnp.sum(inverse_block * point_side[:, None, :, :], axis=2)
    errors = (residual_rows - jnp.sum(point_rows * solved[:, None, None, :, :], axis=3)) * masked
    returned = jnp.sum(cam_rows * errors[:, :, :, None, :], axis=2)
    spread = jnp.einsum("bsjp,bscp->bsjc", returned, selector, precision=lax.Precision.HIGHEST)
    spread = spread.reshape(blocks * slots, 9 * cameras)
    return total + jax.ops.segment_sum(spread, index_tile.reshape(-1), num_segments=total.shape[0])


def local_product(window, jac_cam, jac_point, index_cam, index_tile, live, inverse):
    tiles = jac_cam.shape[0]
    block = math.gcd(tiles, 8)
    turns = tiles // block

    def split(array):
        return array.reshape((turns, block) + array.shape[1:])

    items = (
        split(jac_cam),
        split(jac_point),
        split(index_cam),
        split(index_tile),
        split(live),
        split(inverse),
    )

    def advance(total, item):
        return (block_term(window, total, item), None)

    total, unused = lax.scan(advance, jnp.zeros(window.shape, jnp.float32), items)
    return total


def camera_product(vector, damp_cam, jac_cam, jac_point, index_cam, index_tile, live, inverse):
    group_tiles = lax.axis_size("pts") * vector.shape[1]
    halfway = group_tiles // 2
    panel = lax.all_gather(vector, "pts", axis=1, tiled=True)
    lower = from_behind(panel, "cam", 1)
    upper = from_behind(panel, "cam", -1)
    window = jnp.concatenate([lower[:, halfway:], panel, upper[:, :halfway]], axis=1)
    partial_value = local_product(
        window[0], jac_cam, jac_point, index_cam, index_tile, live, inverse
    )[None]
    from_above = from_behind(partial_value[:, :halfway], "cam", -1)
    from_below = from_behind(partial_value[:, halfway + group_tiles :], "cam", 1)
    summed = partial_value[:, halfway : halfway + group_tiles] + jnp.concatenate(
        [from_below, from_above], axis=1
    )
    return lax.psum_scatter(summed, "pts", scatter_dimension=1, tiled=True) + damp_cam * vector


def on_device(rhs, damp_cam, precond, cam_jac, pt_jac, damp_pt, cam_index, tile_ids, counts):
    slots = cam_jac.shape[2]
    live = (lax.iota(jnp.int32, slots)[None, :] < counts[0][:, None]).astype(jnp.float32)
    inverse = point_inverse(pt_jac[0], counts[0], damp_pt[0])

    def norm_total(residual, scaled):
        return lax.psum(jnp.sum(residual * scaled), ("pts", "cam"))

    solution = jnp.zeros(rhs.shape, jnp.float32)
    residual = rhs
    scaled = precond * residual
    direction = scaled
    energy = norm_total(residual, scaled)
    for iteration in range(ITERS):
        mapped = camera_product(
            direction, damp_cam, cam_jac[0], pt_jac[0], cam_index[0], tile_ids[0], live, inverse
        )
        step_size = energy / lax.psum(jnp.sum(direction * mapped), ("pts", "cam"))
        solution = solution + step_size * direction
        residual = residual - step_size * mapped
        if iteration + 1 < ITERS:
            scaled = precond * residual
            energy_next = norm_total(residual, scaled)
            direction = scaled + energy_next / energy * direction
            energy = energy_next
    return (solution, residual)


def solution(mesh):
    return jax.shard_map(
        on_device,
        mesh=mesh,
        in_specs=(
            P("cam", "pts", None),
            P("cam", "pts", None),
            P("cam", "pts", None),
            P("cam", "pts", None, None, None),
            P("cam", "pts", None, None, None),
            P("cam", "pts", None, None),
            P("cam", "pts", None, None),
            P("cam", "pts", None),
            P("cam", "pts"),
        ),
        out_specs=(P("cam", "pts", None), P("cam", "pts", None)),
        check_vma=False,
    )
```

profile of v0, /device:TPU:1, one launch (start us, length us, event | category | flops | bytes accessed | tf_op | source)
XLA Modules:
  0.0 1812.4 jit_solution(11245703077444273129)
XLA Ops:
  8.6 48.1 %all_gather.9 = f32[1,256,576]{2,0,1:T(1,128)S(1)} all-gather(f32[1,8,576]{2,0,1:T(1,128)S(1)} %copy.194), channel_id=1, replica_groups=mesh['pts'=32,'cam'=8] {'pts'}, dimensions={1}, use_global_device_ids=true | all-gather | bytes 608256 | tf_op jit(solution)/shard_map/all_gather | solution.py:87
  58.4 2.4 collective-permute-start.1
  60.9 2.0 broadcast_multiply_fusion.3
  63.3 2.3 multiply_reduce_fusion.12
  70.1 1.8 fusion.19
  71.9 2.3 collective-permute-done
  75.9 133.3 %while.30 = (s32[]{:T(128)}, f32[512,576]{1,0:T(8,128)S(1)}, s32[12,8,8]{2,1,0:T(8,128)}, f32[12,8,8,18,128]{4,2,3,1,0:T(8,128)}, f32[512,576]{1,0:T(8,128)S(1)}...) while((s32[]{:T(128)}, f32[512,576]{1,0:T(8,128)S(1)}, ...), condition=%wide.region_12.14_spmd, body=%wide.region_4.13_spmd.sunk | while | flops 115127872 | bytes 7966729 | solution.py:80
  94.6 1.7 fusion.61
  116.9 1.7 fusion.61
  128.0 1.7 fusion.61
  139.1 1.7 fusion.61
  150.2 1.7 fusion.61
  161.3 1.7 fusion.61
  183.5 1.7 fusion.61
  205.7 1.7 fusion.61
  209.6 3.6 collective-permute-start.3
  213.2 6.7 collective-permute-done.2
  222.1 258.9 %all-reduce.8.cloned.1.call-done = f32[1,256,576]{2,1,0:T(8,128)} async-done(((f32[1,256,576]{2,1,0:T(8,128)}), f32[1,256,576]{2,1,0:T(8,128)}) %all-reduce.8.cloned.1.call-update) | async-done | bytes 589840
  482.4 76.9 %all-reduce.3 = (f32[]{:T(128)}, f32[]{:T(128)}) all-reduce(f32[]{:T(128)} %get-tuple-element.264, f32[]{:T(128)} %get-tuple-element.263), channel_id=1, replica_groups=mesh['pts'=32,'cam'=8] {'pts','cam'}, use_global_device_ids=true, to_apply=%region_1.2 | all-reduce | flops 2 | bytes 16 | tf_op jit(solution)/shard_map/psum | solution.py:108
  560.5 2.0 multiply_reduce_fusion.16
  562.5 72.7 %psum.44 = f32[]{:T(128)} all-reduce(f32[]{:T(128)} %get-tuple-element.336), channel_id=1, replica_groups=mesh['pts'=32,'cam'=8] {'pts','cam'}, use_global_device_ids=true, to_apply=%region_17.19 | all-reduce | flops 1 | bytes 8 | tf_op jit(solution)/shard_map/psum | solution.py:108
  637.0 41.6 %all_gather.10 = f32[1,256,576]{2,0,1:T(1,128)S(1)} all-gather(f32[1,8,576]{2,0,1:T(1,128)S(1)} %copy.200), channel_id=1, replica_groups=mesh['pts'=32,'cam'=8] {'pts'}, dimensions={1}, use_global_device_ids=true | all-gather | bytes 608256 | tf_op jit(solution)/shard_map/all_gather | solution.py:87
  679.4 3.3 collective-permute-start.5
  682.7 13.3 collective-permute-done.4
  696.7 133.3 %while.31 = (s32[]{:T(128)}, f32[512,576]{1,0:T(8,128)S(1)}, s32[12,8,8]{2,1,0:T(8,128)}, f32[12,8,8,18,128]{4,2,3,1,0:T(8,128)}, f32[512,576]{1,0:T(8,128)S(1)}...) while((s32[]{:T(128)}, f32[512,576]{1,0:T(8,128)S(1)}, ...), condition=%wide.region_26.28_spmd, body=%wide.region_18.27_spmd.sunk | while | flops 115127872 | bytes 7966729 | solution.py:80
  704.4 1.7 fusion.66
  715.5 1.7 fusion.66
  726.6 1.7 fusion.66
  737.7 1.7 fusion.66
  748.8 1.7 fusion.66
  759.9 1.7 fusion.66
  782.2 1.7 fusion.66
  793.3 1.7 fusion.66
  815.5 1.7 fusion.66
  830.2 3.6 collective-permute-start.7
  833.8 6.7 collective-permute-done.6
  841.5 261.5 %all-reduce.10.cloned.1.call-done = f32[1,256,576]{2,1,0:T(8,128)} async-done(((f32[1,256,576]{2,1,0:T(8,128)}), f32[1,256,576]{2,1,0:T(8,128)}) %all-reduce.10.cloned.1.call-update) | async-done | bytes 589840
  1104.3 76.8 %psum.45 = f32[]{:T(128)} all-reduce(f32[]{:T(128)} %multiply_reduce_fusion.15), channel_id=1, replica_groups=mesh['pts'=32,'cam'=8] {'pts','cam'}, use_global_device_ids=true, to_apply=%region_29.31 | all-reduce | flops 1 | bytes 8 | tf_op jit(solution)/shard_map/psum | solution.py:119
  1182.3 1.9 multiply_reduce_fusion.14
  1184.2 72.8 %psum.46 = f32[]{:T(128)} all-reduce(f32[]{:T(128)} %get-tuple-element.333), channel_id=1, replica_groups=mesh['pts'=32,'cam'=8] {'pts','cam'}, use_global_device_ids=true, to_apply=%region_31.33 | all-reduce | flops 1 | bytes 8 | tf_op jit(solution)/shard_map/psum | solution.py:108
  1259.0 41.7 %all_gather.11 = f32[1,256,576]{2,0,1:T(1,128)S(1)} all-gather(f32[1,8,576]{2,0,1:T(1,128)S(1)} %copy.205), channel_id=1, replica_groups=mesh['pts'=32,'cam'=8] {'pts'}, dimensions={1}, use_global_device_ids=true | all-gather | bytes 608256 | tf_op jit(solution)/shard_map/all_gather | solution.py:87
  1301.5 3.3 collective-permute-start.9
  1304.8 13.3 collective-permute-done.8
  1318.8 133.3 %while.32 = (s32[]{:T(128)}, f32[512,576]{1,0:T(8,128)S(1)}, s32[12,8,8]{2,1,0:T(8,128)}, f32[12,8,8,18,128]{4,2,3,1,0:T(8,128)}, f32[512,576]{1,0:T(8,128)S(1)}...) while((s32[]{:T(128)}, f32[512,576]{1,0:T(8,128)S(1)}, ...), condition=%wide.region_40.42_spmd, body=%wide.region_32.41_spmd.sunk | while | flops 115127872 | bytes 7966729 | solution.py:80
  1452.3 3.6 collective-permute-start.11
  1455.9 6.7 collective-permute-done.10
  1463.5 261.5 %all-reduce.12.cloned.1.call-done = f32[1,256,576]{2,1,0:T(8,128)} async-done(((f32[1,256,576]{2,1,0:T(8,128)}), f32[1,256,576]{2,1,0:T(8,128)}) %all-reduce.12.cloned.1.call-update) | async-done | bytes 589840
  1726.4 76.8 %psum.47 = f32[]{:T(128)} all-reduce(f32[]{:T(128)} %multiply_reduce_fusion.13), channel_id=1, replica_groups=mesh['pts'=32,'cam'=8] {'pts','cam'}, use_global_device_ids=true, to_apply=%region_43.45 | all-reduce | flops 1 | bytes 8 | tf_op jit(solution)/shard_map/psum | solution.py:119
  (1064 shorter events, 390.3 us)
Async XLA Ops:
  7.2 53.6 %copy-start.19 = (s32[1,96]{1,0:T(1,128)S(1)}, s32[1,96]{1,0:T(1,128)}, u32[]{:S(2)}) copy-start(s32[1,96]{1,0:T(1,128)} %param.25) | copy-start | bytes 1156
  7.2 473.9 %all-reduce.8.cloned.1.call-start = ((), (), s32[]{:S(2)}) async-start(), calls=%async_computation | async-start | bytes 1310720
  8.0 0.6 copy-start.7
  57.2 17.1 collective-permute-start
  58.4 16.8 collective-permute-start.1
  60.9 2.4 copy-start
  63.3 2.3 copy-start.15
  67.1 1.6 copy-start.18
  209.2 10.6 collective-permute-start.2
  209.5 11.4 copy-start.20
  209.5 271.5 %copy-start.1 = (f32[1,8,576]{2,1,0:T(8,128)S(1)}, f32[1,8,576]{2,1,0:T(8,128)}, u32[]{:S(2)}) copy-start(f32[1,8,576]{2,1,0:T(8,128)} %param.18) | copy-start | bytes 55300
  209.5 271.5 %copy-start.8 = (f32[1,8,576]{2,1,0:T(8,128)S(1)}, f32[1,8,576]{2,1,0:T(8,128)}, u32[]{:S(2)}) copy-start(f32[1,8,576]{2,1,0:T(8,128)} %copy-done.7) | copy-start | bytes 55300
  209.6 271.5 %copy-start.14 = (f32[1,8,576]{2,1,0:T(8,128)S(1)}, f32[1,8,576]{2,1,0:T(8,128)}, u32[]{:S(2)}) copy-start(f32[1,8,576]{2,1,0:T(8,128)} %param.17) | copy-start | bytes 55300
  209.6 351.0 %copy-start.12 = (f32[1,8,576]{2,1,0:T(8,128)S(1)}, f32[1,8,576]{2,1,0:T(8,128)}, u32[]{:S(2)}) copy-start(f32[1,8,576]{2,1,0:T(8,128)} %param.19) | copy-start | bytes 55300
  209.6 10.3 collective-permute-start.3
  220.8 882.2 %all-reduce.10.cloned.1.call-start = ((), (), s32[]{:S(2)}) async-start(), calls=%async_computation.1 | async-start | bytes 1310720
  636.4 0.6 copy-start.4
  679.1 17.0 collective-permute-start.4
  679.4 16.7 collective-permute-start.5
  830.1 10.4 collective-permute-start.6
  830.2 272.8 %copy-start.2 = (f32[1,8,576]{2,1,0:T(8,128)S(1)}, f32[1,8,576]{2,1,0:T(8,128)}, u32[]{:S(2)}) copy-start(f32[1,8,576]{2,1,0:T(8,128)} %param.18) | copy-start | bytes 55300
  830.2 272.8 %copy-start.5 = (f32[1,8,576]{2,1,0:T(8,128)S(1)}, f32[1,8,576]{2,1,0:T(8,128)}, u32[]{:S(2)}) copy-start(f32[1,8,576]{2,1,0:T(8,128)} %copy-done.4) | copy-start | bytes 55300
  830.2 352.1 %copy-start.13 = (f32[1,8,576]{2,1,0:T(8,128)S(1)}, f32[1,8,576]{2,1,0:T(8,128)}, u32[]{:S(2)}) copy-start(f32[1,8,576]{2,1,0:T(8,128)} %param.19) | copy-start | bytes 55300
  830.2 352.1 %copy-start.16 = (f32[1,8,576]{2,1,0:T(8,128)S(1)}, f32[1,8,576]{2,1,0:T(8,128)}, u32[]{:S(2)}) copy-start(f32[1,8,576]{2,1,0:T(8,128)} %get-tuple-element.338) | copy-start | bytes 55300
  830.2 10.3 collective-permute-start.7
  841.5 883.6 %all-reduce.12.cloned.1.call-start = ((), (), s32[]{:S(2)}) async-start(), calls=%async_computation.2 | async-start | bytes 1310720
  1258.4 0.6 copy-start.10
  1301.1 17.0 collective-permute-start.8
  1301.5 16.7 collective-permute-start.9
  1452.2 10.4 collective-permute-start.10
  1452.3 272.8 %copy-start.3 = (f32[1,8,576]{2,1,0:T(8,128)S(1)}, f32[1,8,576]{2,1,0:T(8,128)}, u32[]{:S(2)}) copy-start(f32[1,8,576]{2,1,0:T(8,128)} %param.18) | copy-start | bytes 55300
  1452.3 272.8 %copy-start.11 = (f32[1,8,576]{2,1,0:T(8,128)S(1)}, f32[1,8,576]{2,1,0:T(8,128)}, u32[]{:S(2)}) copy-start(f32[1,8,576]{2,1,0:T(8,128)} %copy-done.10) | copy-start | bytes 55300
  1452.3 352.2 %copy-start.6 = (f32[1,8,576]{2,1,0:T(8,128)S(1)}, f32[1,8,576]{2,1,0:T(8,128)}, u32[]{:S(2)}) copy-start(f32[1,8,576]{2,1,0:T(8,128)} %copy-done.4) | copy-start | bytes 55300
  1452.3 352.2 %copy-start.9 = (f32[1,8,576]{2,1,0:T(8,128)S(1)}, f32[1,8,576]{2,1,0:T(8,128)}, u32[]{:S(2)}) copy-start(f32[1,8,576]{2,1,0:T(8,128)} %copy-done.7) | copy-start | bytes 55300
  1452.3 352.2 %copy-start.17 = (f32[1,8,576]{2,1,0:T(8,128)S(1)}, f32[1,8,576]{2,1,0:T(8,128)}, u32[]{:S(2)}) copy-start(f32[1,8,576]{2,1,0:T(8,128)} %get-tuple-element.335) | copy-start | bytes 55300
  1452.3 10.3 collective-permute-start.11
Sparse Core Ops, SparseCore 0:
  221.0 260.0 all-reduce.7
  841.6 261.3 all-reduce.9
  1463.7 261.3 all-reduce.11
where the time goes:
time: 1820 us; the launch traced here: 1810 us
  waiting for transfers between devices  831 us (46%)
  blocking collectives  507 us (28%)
  other arithmetic  181 us (10%)
  local copies, waits for them, and re-layouts  143 us (8%)
  matrix products  103 us (6%)
  starting transfers between devices  22.3 us (1%)
  between operations  21.4 us (1%)
    unnamed x6, waiting for transfers between devices  782 us
    psum x3, blocking collectives, norm_total(): return lax.psum(jnp.sum(residual * scaled), ('pts', 'cam'))  222 us
    psum x2, blocking collectives, on_device(): step_size = energy / lax.psum(jnp.sum(direction * mapped), ('pts', 'cam'))  154 us
    all_gather x3, blocking collectives, camera_product(): panel = lax.all_gather(vector, 'pts', axis=1, tiled=True)  131 us
    dot_general x36, matrix products, block_term(): jnp.einsum('bsjp,bscp->bsjc', returned, selector, precision=lax.Precision...  62.4 us
    scatter-add x36, other arithmetic, block_term(): jax.ops.segment_sum(spread, index_tile.reshape(-1), num_segments=total.sh...  53.7 us
    ppermute x12, waiting for transfers between devices, from_behind(): lax.ppermute(shard, axis, [(i, (i + by) % devices) for i in range(devices)])  49 us
    dot_general x36, matrix products, block_term(): jnp.einsum('bsjc,bscp->bsjp', picked_tiles, selector, precision=lax.Preci...  40.3 us
  transfers between devices with their start and end apart: 15, of which 9 were waited for; matrix products, arithmetic and copies ran while one was open for 1% of the time, Pallas kernels for 0%

commit v1 on v0

v1 whole, which is shorter than its diff:
```python
import functools

import jax
import jax.numpy as jnp
from jax import lax
from jax.experimental import pallas as pl
from jax.experimental.pallas import tpu as pltpu
from jax.sharding import PartitionSpec as P

ITERS = 3
CPAR = 9
CAMS = 64
LANES = 128
SCALE = 0.125
MESH = pl.DeviceIdType.MESH
F32 = jnp.float32
BF16 = jnp.bfloat16
NT = (((1,), (1,)), ((), ()))
NN = (((1,), (0,)), ((), ()))


def mm(a, b, dims):
    return lax.dot_general(a, b, dims, preferred_element_type=F32)


def split_two(x):
    hi = x.astype(BF16)
    return hi, (x - hi.astype(F32)).astype(BF16)


def kernel(
    n_pts, n_cam, tiles, slots, ct,
    rhs_ref, damp_ref, precond_ref, ids_col_ref, ids_row_ref, counts_ref,
    cam_jac_ref, pt_jac_ref, damp_pt_ref, cam_index_ref,
    sol_ref, res_ref,
    jac, pjac, dpt, cidx, inv, sel, pick_hot, sum_hot, picked, spread, win_split,
    win, acc, got, mixed, parts, vecs, bases, scal_cam, scal_pts,
    in_sem, wsend, wrecv, fsend, frecv, psend, precv, rsend, rrecv, csend, crecv, osend, orecv,
):
    half = n_pts // 2
    chips = half * n_cam
    reach = half // 2
    span = 2 * reach + 1
    rows = span * 2 * ct
    width = 5 * LANES
    pairs = tiles * slots
    d = lax.axis_index("pts")
    g = lax.axis_index("cam")
    core = lax.rem(d, 2)
    other = 1 - core
    chip = g * half + d // 2

    def at_offset(offset):
        place = lax.rem(chip + (offset + chips), chips)
        return {"pts": lax.rem(place, half) * 2 + core, "cam": place // half}

    partner = {"pts": d + 1 - 2 * core, "cam": g}
    offsets = []
    for far in range(reach, 0, -1):
        offsets += [far, -far]

    loads = [
        pltpu.make_async_copy(pt_jac_ref.at[0], pjac.at[:, :, pl.ds(0, 6), :], in_sem.at[0]),
        pltpu.make_async_copy(damp_pt_ref.at[0], dpt.at[:, pl.ds(0, 3), :], in_sem.at[1]),
        pltpu.make_async_copy(cam_index_ref.at[0], cidx, in_sem.at[2]),
        pltpu.make_async_copy(cam_jac_ref.at[0], jac.at[:, :, pl.ds(0, 2 * CPAR), :], in_sem.at[3]),
    ]
    for load in loads:
        load.start()

    barrier = pltpu.get_barrier_semaphore()

    def greet(device):
        pl.semaphore_signal(barrier, inc=1, device_id=device, device_id_type=MESH)

    for offset in offsets:
        greet(at_offset(offset))
    greet(partner)
    for i in range(1, n_cam):
        greet({"pts": d, "cam": lax.rem(g + i, n_cam)})
    for i in range(1, n_pts):
        greet({"pts": lax.rem(d + i, n_pts), "cam": g})
    pl.semaphore_wait(barrier, len(offsets) + 1 + (n_cam - 1) + (n_pts - 1))

    def send(src, dst, ssem, rsem, device):
        copy = pltpu.make_async_remote_copy(
            src_ref=src, dst_ref=dst, send_sem=ssem, recv_sem=rsem, device_id=device, device_id_type=MESH
        )
        copy.start()
        return copy

    def start_gather(p, value):
        win[p, reach, core] = value
        copies = []
        for offset in offsets:
            slot = reach - offset
            copies.append(
                send(win.at[p, reach, core], win.at[p, slot, core], wsend.at[p, slot], wrecv.at[p, slot], at_offset(offset))
            )
        copies.append(
            send(win.at[p, reach, core], win.at[p, reach, core], fsend.at[p, reach], frecv.at[p, reach], partner)
        )
        return copies

    def finish_gather(p, copies):
        forwards = [copies.pop()]
        for offset, copy in reversed(list(zip(offsets, copies))):
            copy.wait_recv()
            slot = reach - offset
            forwards.append(
                send(win.at[p, slot, core], win.at[p, slot, core], fsend.at[p, slot], frecv.at[p, slot], partner)
            )
        for copy in copies:
            copy.wait_send()
        for copy in forwards:
            copy.wait()

    def reduce_blocks(p):
        swaps = []
        order = offsets + [0]
        for offset in order:
            b = reach + offset
            swaps.append(send(acc.at[p, b, other], got.at[p, b], psend.at[p, b], precv.at[p, b], partner))
        copies = []
        for offset, swap in zip(order, swaps):
            b = reach + offset
            swap.wait_recv()
            total = acc[p, b, core] + got[p, b]
            if offset:
                mixed[p, b] = total
                copies.append(send(mixed.at[p, b], parts.at[p, b], rsend.at[p, b], rrecv.at[p, b], at_offset(offset)))
        for offset, copy in zip(offsets, copies):
            copy.wait_recv()
            total = total + parts[p, reach + offset]
        for swap in swaps:
            swap.wait_send()
        for copy in copies:
            copy.wait_send()
        return total

    def wide(value):
        return jnp.concatenate([value, jnp.zeros((ct, width - value.shape[1]), F32)], axis=1)

    sub = lax.broadcasted_iota(jnp.int32, (slots, LANES), 0)
    lane = lax.broadcasted_iota(jnp.int32, (slots, LANES), 1)
    even = lax.rem(sub, 2) == 0
    low = lane < CAMS
    straight = even == low

    rhs = wide(rhs_ref[0])
    damp = wide(damp_ref[0])
    precond = wide(precond_ref[0])
    vecs[0] = rhs
    scaled = precond * rhs
    bases[0] = scaled
    copies = start_gather(0, scaled)

    shift = (d // 2) * (2 * ct)
    spot = lax.broadcasted_iota(jnp.int32, (16, width), 1)
    spot = jnp.where(spot < rows, spot, spot - rows)

    def pick_rows(i, carry):
        ids = ids_col_ref[pl.ds(i * 16, 16), :] - shift
        hot = jnp.where(spot == ids, 1.0, 0.0).astype(BF16)
        pick_hot[pl.ds(i * 16, 16), :] = hot
        return carry

    lax.fori_loop(0, pairs // 16, pick_rows, 0)
    high = lax.broadcasted_iota(jnp.int32, (16, pairs), 0)

    def sum_rows(i, carry):
        ids = ids_row_ref[...] - shift - i * 16
        hot = jnp.where(high == ids, 1.0, 0.0).astype(BF16)
        sum_hot[pl.ds(i * 16, 16), pl.ds(0, pairs)] = hot
        sum_hot[pl.ds(i * 16, 16), pl.ds(pairs, pairs)] = hot
        return carry

    lax.fori_loop(0, rows // 16, sum_rows, 0)
    loads[0].wait()
    loads[1].wait()
    loads[2].wait()
    jflat = jac.reshape(tiles * slots * 24, LANES)
    pflat = pjac.reshape(tiles * slots * 8, LANES)

    def live_of(t):
        return sub < counts_ref[0, t]

    def point_rows(t):
        return [pflat[pl.ds(t * slots * 8 + r, slots, stride=8), :] for r in range(6)]

    camera = lax.broadcasted_iota(jnp.int32, (CAMS, LANES), 0)

    def prepare(t, carry):
        live = live_of(t)
        p = [jnp.where(live, row, 0.0) for row in point_rows(t)]

        def entry(a, b):
            value = jnp.sum(p[a] * p[b] + p[3 + a] * p[3 + b], axis=0, keepdims=True)
            if a == b:
                value = value + dpt[t, pl.ds(a, 1), :]
            return value

        v00, v01, v02 = entry(0, 0), entry(0, 1), entry(0, 2)
        v11, v12, v22 = entry(1, 1), entry(1, 2), entry(2, 2)
        c00 = v11 * v22 - v12 * v12
        c01 = v12 * v02 - v01 * v22
        c02 = v01 * v12 - v11 * v02
        c11 = v22 * v00 - v02 * v02
        c12 = v02 * v01 - v00 * v12
        c22 = v00 * v11 - v01 * v01
        det = v00 * c00 + v01 * c01 + v02 * c02
        for i, value in enumerate((c00, c01, c02, c11, c12, c22)):
            inv[t, pl.ds(i, 1), :] = value / det
        for k in range(slots):
            index = cidx[t, pl.ds(k, 1), :]
            sel[t, pl.ds(k * CAMS, CAMS), :] = jnp.where(camera == index, 1.0, 0.0).astype(BF16)
        return carry

    lax.fori_loop(0, tiles, prepare, 0)
    loads[3].wait()

    def tile_term(t):
        live = live_of(t)
        index = cidx[t]
        above = index + CAMS
        j_rows = [jflat[pl.ds(t * slots * 24 + r, slots, stride=24), :] for r in range(2 * CPAR)]
        p = point_rows(t)
        found = []
        for j in range(CPAR):
            table = picked[pl.ds(t * slots, slots), pl.ds((j // 2) * LANES, LANES)]
            found.append(
                jnp.take_along_axis(table, above if j % 2 else index, axis=1, mode="promise_in_bounds")
            )
        q = []
        for r in range(2):
            total = j_rows[CPAR * r] * found[0]
            for j in range(1, CPAR):
                total = total + j_rows[CPAR * r + j] * found[j]
            q.append(jnp.where(live, total, 0.0))
        y = [jnp.sum(p[a] * q[0] + p[3 + a] * q[1], axis=0, keepdims=True) for a in range(3)]
        m = [inv[t, pl.ds(i, 1), :] for i in range(6)]
        z = [
            m[0] * y[0] + m[1] * y[1] + m[2] * y[2],
            m[1] * y[0] + m[3] * y[1] + m[4] * y[2],
            m[2] * y[0] + m[4] * y[1] + m[5] * y[2],
        ]
        e = []
        for r in range(2):
            back = p[3 * r] * z[0] + p[3 * r + 1] * z[1] + p[3 * r + 2] * z[2]
            e.append(jnp.where(live, q[r] - back, 0.0))
        given = jnp.concatenate([j_rows[j] * e[0] + j_rows[CPAR + j] * e[1] for j in range(CPAR)], axis=0)
        hi, lo = split_two(given)
        hots = sel[t]
        out = mm(jnp.concatenate([hi, lo], axis=1), jnp.concatenate([hots, hots], axis=1), NT)

        def diagonal(j):
            block = [out[j * slots : (j + 1) * slots, i * LANES : (i + 1) * LANES] for i in range(slots // 2)]
            value = block[-1]
            for i in range(slots // 2 - 2, -1, -1):
                value = jnp.where(sub < 2 * (i + 1), block[i], value)
            return value

        merged = []
        for i in range(0, CPAR, 2):
            first = diagonal(i)
            second = diagonal(i + 1) if i + 1 < CPAR else jnp.zeros_like(first)
            crossed = pltpu.roll(jnp.where(even, second, first), CAMS, 1)
            merged.append(jnp.where(straight, jnp.where(even, first, second), crossed))
        return jnp.concatenate(merged, axis=1)

    together = 4

    def tile_step(i, carry):
        terms = [tile_term(i * together + u) for u in range(together)]
        for u in range(0, together, 2):
            hi, lo = split_two(jnp.concatenate(terms[u : u + 2], axis=0))
            start = pl.multiple_of((i * together + u) * slots, 16)
            spread[pl.ds(start, 16), :] = hi
            spread[pl.ds(pairs + start, 16), :] = lo
        return carry

    for p in range(ITERS):
        finish_gather(p, copies)
        window = win[p].reshape(rows, width)
        hi, lo = split_two(window)
        win_split[pl.ds(0, rows), :] = hi
        win_split[pl.ds(rows, rows), :] = lo

        def pick(i, carry):
            start = pl.multiple_of(i * LANES, LANES)
            picked[pl.ds(start, LANES), :] = mm(pick_hot[pl.ds(start, LANES), pl.ds(0, 2 * rows)], win_split[...], NN)
            return carry

        lax.fori_loop(0, pairs // LANES, pick, 0)
        lax.fori_loop(0, tiles // together, tile_step, 0)
        for i in range(5):
            cut = pl.ds(i * LANES, LANES)
            value = mm(sum_hot[...], spread[:, cut], NN)
            acc[p, :, :, :, cut] = value.reshape(span, 2, ct, LANES)
        total = reduce_blocks(p)
        mapped = SCALE * (total + damp * bases[p])
        vecs[p + 1] = mapped
        if p + 1 < ITERS:
            scaled = precond * mapped
            bases[p + 1] = scaled
            copies = start_gather(p + 1, scaled)

    wanted = [(i, j) for i in range(ITERS) for j in range(i, ITERS + 1)]
    lines = []
    for i, j in wanted:
        product = bases[i] * vecs[j]
        line = product[:, :LANES]
        for n in range(1, 5):
            line = line + product[:, n * LANES : (n + 1) * LANES]
        lines.append(jnp.sum(line, axis=0, keepdims=True))
    lines.append(jnp.zeros((16 - len(lines), LANES), F32))
    scal_cam[g] = jnp.concatenate(lines, axis=0)
    copies = [
        send(scal_cam.at[g], scal_cam.at[g], csend.at[i], crecv.at[i], {"pts": d, "cam": lax.rem(g + i, n_cam)})
        for i in range(1, n_cam)
    ]
    for copy in copies:
        copy.wait()
    total = scal_cam[0]
    for i in range(1, n_cam):
        total = total + scal_cam[i]
    scal_pts[d] = total
    copies = [
        send(scal_pts.at[d], scal_pts.at[d], osend.at[i], orecv.at[i], {"pts": lax.rem(d + i, n_pts), "cam": g})
        for i in range(1, n_pts)
    ]
    for copy in copies:
        copy.wait()
    total = scal_pts[0]
    for i in range(1, n_pts):
        total = total + scal_pts[i]
    sums = jnp.broadcast_to(jnp.sum(total, axis=1, keepdims=True), (16, LANES))
    gram = {}
    for i, (a, b) in enumerate(wanted):
        gram[a, b] = gram[b, a] = sums[i : i + 1, :]

    one = jnp.ones((1, LANES), F32)
    nil = jnp.zeros((1, LANES), F32)
    x = [nil] * ITERS
    r = [one] + [nil] * ITERS
    s = [one] + [nil] * (ITERS - 1)
    energy = gram[0, 0]
    for p in range(ITERS):
        mapped = [nil] + [value * (1.0 / SCALE) for value in s]
        steep = nil
        for i in range(p + 1):
            row = nil
            for j in range(1, p + 2):
                row = row + mapped[j] * gram[i, j]
            steep = steep + s[i] * row
        step = energy / steep
        x = [a + step * b for a, b in zip(x, s)]
        r = [a - step * b for a, b in zip(r, mapped)]
        if p + 1 < ITERS:
            following = nil
            for i in range(p + 2):
                row = nil
                for j in range(p + 2):
                    row = row + r[j] * gram[i, j]
                following = following + r[i] * row
            ratio = following / energy
            s = [a + ratio * b for a, b in zip(r[:ITERS], s)]
            energy = following

    def spread_out(value):
        return jnp.broadcast_to(value[:, :1], (ct, width))

    solution_value = spread_out(x[0]) * bases[0]
    residual_value = spread_out(r[0]) * vecs[0]
    for i in range(1, ITERS):
        solution_value = solution_value + spread_out(x[i]) * bases[i]
    for i in range(1, ITERS + 1):
        residual_value = residual_value + spread_out(r[i]) * vecs[i]
    sol_ref[0] = solution_value[:, : CPAR * CAMS]
    res_ref[0] = residual_value[:, : CPAR * CAMS]


def solution(mesh):
    n_pts, n_cam = mesh.shape["pts"], mesh.shape["cam"]

    def on_device(rhs, damp_cam, precond, cam_jac, pt_jac, damp_pt, cam_index, tile_ids, counts):
        ct = rhs.shape[1]
        tiles, slots = cam_jac.shape[1:3]
        pairs = tiles * slots
        span = n_pts // 2 + 1
        rows = span * 2 * ct
        width = 5 * LANES
        vmem = pl.BlockSpec(memory_space=pltpu.VMEM)
        anywhere = pl.BlockSpec(memory_space=pl.ANY)
        dma = pltpu.SemaphoreType.DMA
        shape = jax.ShapeDtypeStruct(rhs.shape, F32)
        return pl.pallas_call(
            functools.partial(kernel, n_pts, n_cam, tiles, slots, ct),
            out_shape=(shape, shape),
            in_specs=[vmem] * 5 + [pl.BlockSpec(memory_space=pltpu.SMEM)] + [anywhere] * 4,
            out_specs=(vmem, vmem),
            scratch_shapes=[
                pltpu.VMEM((tiles, slots, 24, LANES), F32),
                pltpu.VMEM((tiles, slots, 8, LANES), F32),
                pltpu.VMEM((tiles, 8, LANES), F32),
                pltpu.VMEM((tiles, slots, LANES), jnp.int32),
                pltpu.VMEM((tiles, 8, LANES), F32),
                pltpu.VMEM((tiles, slots * CAMS, LANES), BF16),
                pltpu.VMEM((pairs, width), BF16),
                pltpu.VMEM((rows, 2 * pairs), BF16),
                pltpu.VMEM((pairs, width), F32),
                pltpu.VMEM((2 * pairs, width), BF16),
                pltpu.VMEM((2 * rows, width), BF16),
                pltpu.VMEM((ITERS, span, 2, ct, width), F32),
                pltpu.VMEM((ITERS, span, 2, ct, width), F32),
                pltpu.VMEM((ITERS, span, ct, width), F32),
                pltpu.VMEM((ITERS, span, ct, width), F32),
                pltpu.VMEM((ITERS, span, ct, width), F32),
                pltpu.VMEM((ITERS + 1, ct, width), F32),
                pltpu.VMEM((ITERS, ct, width), F32),
                pltpu.VMEM((n_cam, 16, LANES), F32),
                pltpu.VMEM((n_pts, 16, LANES), F32),
                dma((4,)),
            ]
            + [dma((ITERS, span))] * 8
            + [dma((n_cam,)), dma((n_cam,)), dma((n_pts,)), dma((n_pts,))],
            compiler_params=pltpu.CompilerParams(
                collective_id=0, has_side_effects=True, vmem_limit_bytes=62_000_000
            ),
        )(
            rhs, damp_cam, precond, tile_ids.reshape(pairs, 1), tile_ids.reshape(1, pairs), counts,
            cam_jac, pt_jac, damp_pt, cam_index,
        )

    return jax.shard_map(
        on_device,
        mesh=mesh,
        in_specs=(
            P("cam", "pts", None),
            P("cam", "pts", None),
            P("cam", "pts", None),
            P("cam", "pts", None, None, None),
            P("cam", "pts", None, None, None),
            P("cam", "pts", None, None),
            P("cam", "pts", None, None),
            P("cam", "pts", None),
            P("cam", "pts"),
        ),
        out_specs=(P("cam", "pts", None), P("cam", "pts", None)),
        check_vma=False,
    )
```

time: 1820 us -> 179 us (0.10)
  waiting for transfers between devices: 831 us -> 0 us
  blocking collectives: 507 us -> 0 us
  other arithmetic: 181 us -> 0 us
  Pallas kernels: 0 us -> 159 us
  local copies, waits for them, and re-layouts: 143 us -> 19.3 us
  matrix products: 103 us -> 0 us
  starting transfers between devices: 22.3 us -> 0 us
  between operations: 21.4 us -> 0.64 us
    unnamed x6 -> x0, waiting for transfers between devices: 782 us -> none
    psum x5 -> x0, blocking collectives: 376 us -> none  [the longest x3 222 us: norm_total(): return lax.psum(jnp.sum(residual * scaled), ('pts', 'cam'))]
    pallas_call x0 -> x1, Pallas kernels: none -> 159 us  [on_device(): pl.pallas_call(functools.partial(kernel, n_pts, n_cam, tiles, slots, ct),...]
    all_gather x3 -> x0, blocking collectives: 131 us -> none  [camera_product(): panel = lax.all_gather(vector, 'pts', axis=1, tiled=True)]
    dot_general x72 -> x0, matrix products: 103 us -> none  [the longest x36 62.4 us: block_term(): jnp.einsum('bsjp,bscp->bsjc', returned, selector, precision=lax.Precision...]
    reduce_sum x223 -> x0, other arithmetic: 82 us -> none  [the longest x72 36.2 us: block_term(): jnp.sum(point_rows * residual_rows[:, :, :, None, :], axis=(1, 2))]
    scatter-add x36 -> x0, other arithmetic: 53.7 us -> none  [block_term(): jax.ops.segment_sum(spread, index_tile.reshape(-1), num_segments=total.sh...]
    ppermute x12 -> x0, waiting for transfers between devices: 49 us -> none  [from_behind(): lax.ppermute(shard, axis, [(i, (i + by) % devices) for i in range(devices)])]
  transfers between devices with their start and end apart: 15 -> 0, of which waited for: 9 -> 0; matrix products, arithmetic and copies ran while one was open for 1% -> 0% of each run, Pallas kernels for 0% -> 0%
where the time goes in v1:
time: 179 us; the launch traced here: 178 us
  Pallas kernels  159 us (89%)
  local copies, waits for them, and re-layouts  19.3 us (11%)
    pallas_call x1, Pallas kernels, on_device(): pl.pallas_call(functools.partial(kernel, n_pts, n_cam, tiles, slots, ct),...  159 us
    unnamed x6, local copies, waits for them, and re-layouts  17.7 us

profile of v1, /device:TPU:1, one launch (start us, length us, event | category | flops | bytes accessed | tf_op | source)
XLA Modules:
  0.0 178.5 jit_solution(7490807205847833858)
XLA Ops:
  0.6 0.8 copy.16
  1.4 0.7 reshape.11.ids_row_ref
  2.1 1.7 copy.21.damp_pt_ref
  3.8 0.9 reshape.12.ids_col_ref
  4.7 4.0 %copy.20.pt_jac_ref = f32[1,96,8,6,128]{4,3,2,1,0:T(8,128)} copy(f32[1,96,8,6,128]{4,2,3,1,0:T(8,128)} %param.13) | data formatting | bytes 4718592 | tf_op args[4]
  8.7 8.6 %copy.19.cam_jac_ref = f32[1,96,8,18,128]{4,3,2,1,0:T(8,128)} copy(f32[1,96,8,18,128]{4,2,3,1,0:T(8,128)} %param.12) | data formatting | bytes 14155776 | tf_op args[3]
  17.2 158.5 %shard_map.104 = (f32[1,8,576]{2,1,0:T(8,128)}, f32[1,8,576]{2,1,0:T(8,128)}) custom-call(f32[1,8,576]{2,1,0:T(8,128)} %rhs_ref.1, f32[1,8,576]{2,1,0:T(8,128)} %damp_ref.1, f32[1,8,576]{2,1,0:T(8,128)} %precond_ref.1, s32[768,1]{1,0:T(8,128)} %reshape.12.ids_col_ref, s32[1,768]{1,0:T(1,128)} %reshape.11.ids_row_ref, s32[1,96]{1,0:T(1,128)} %counts_ref.1, ...), custom_call_target="tpu_custom_call" | custom-call | tf_op jit(solution)/shard_map/pallas_call | solution.py:397
  175.8 1.3 copy.24
  177.1 1.3 copy.25

commit v2 on v1

v2 whole, which is shorter than its diff:
```python
import functools

import jax
import jax.numpy as jnp
from jax import lax
from jax.experimental import pallas as pl
from jax.experimental.pallas import tpu as pltpu
from jax.sharding import PartitionSpec as P

ITERS = 3
CPAR = 9
CAMS = 64
LANES = 128
SCALE = 0.125
MESH = pl.DeviceIdType.MESH
F32 = jnp.float32
BF16 = jnp.bfloat16
NT = (((1,), (1,)), ((), ()))
NN = (((1,), (0,)), ((), ()))


def mm(a, b, dims):
    return lax.dot_general(a, b, dims, preferred_element_type=F32)


def split_two(x):
    hi = x.astype(BF16)
    return hi, (x - hi.astype(F32)).astype(BF16)


def kernel(
    n_pts, n_cam, tiles, slots, ct,
    rhs_ref, damp_ref, precond_ref, ids_ref, counts_ref,
    cam_jac_ref, pt_jac_ref, damp_pt_ref, cam_index_ref,
    sol_ref, res_ref,
    jac, pjac, dpt, cidx, inv, sel, pick_hot, sum_hot, picked, spread, win_split, given_split,
    win, acc, got, crossed, crossing, mixed, parts, vecs, bases, scal_cam, scal_pts,
    in_sem, zsend, zrecv, ysend, yrecv, esend, erecv, fsend, frecv,
    asend, arecv, bsend, brecv, rsend, rrecv, csend, crecv, osend, orecv,
):
    layers = n_pts // 4
    quads = layers * n_cam
    reach = layers // 2
    span = 2 * reach + 1
    rows = span * 4 * ct
    width = 5 * LANES
    pairs = tiles * slots
    d = lax.axis_index("pts")
    g = lax.axis_index("cam")
    layer = d // 4
    side = lax.rem(d, 4) // 2
    core = lax.rem(d, 2)
    quad = g * layers + layer

    def at_offset(offset):
        place = lax.rem(quad + (offset + quads), quads)
        return {"pts": lax.rem(place, layers) * 4 + side * 2 + core, "cam": place // layers}

    twin = {"pts": d + 1 - 2 * core, "cam": g}
    across = {"pts": d + 2 - 4 * side, "cam": g}
    offsets = []
    for far in range(reach, 0, -1):
        offsets += [far, -far]
    places = {offset: at_offset(offset) for offset in offsets}

    loads = [
        pltpu.make_async_copy(pt_jac_ref.at[0], pjac, in_sem.at[0]),
        pltpu.make_async_copy(damp_pt_ref.at[0], dpt, in_sem.at[1]),
        pltpu.make_async_copy(cam_index_ref.at[0], cidx, in_sem.at[2]),
        pltpu.make_async_copy(cam_jac_ref.at[0], jac, in_sem.at[3]),
    ]
    for load in loads:
        load.start()

    barrier = pltpu.get_barrier_semaphore()

    def greet(device):
        pl.semaphore_signal(barrier, inc=1, device_id=device, device_id_type=MESH)

    for offset in offsets:
        greet(places[offset])
    for i in range(1, n_cam):
        greet({"pts": d, "cam": lax.rem(g + i, n_cam)})
    for i in range(1, n_pts):
        greet({"pts": lax.rem(d + i, n_pts), "cam": g})
    pl.semaphore_wait(barrier, len(offsets) + (n_cam - 1) + (n_pts - 1))

    def send(src, dst, ssem, rsem, device):
        copy = pltpu.make_async_remote_copy(
            src_ref=src, dst_ref=dst, send_sem=ssem, recv_sem=rsem, device_id=device, device_id_type=MESH
        )
        copy.start()
        return copy

    def forward(p, slot, of_side, ssem, rsem, device):
        block = win.at[p, slot, of_side, core]
        return send(block, block, ssem.at[p, slot], rsem.at[p, slot], device)

    def start_gather(p, value):
        win[p, reach, side, core] = value
        own = win.at[p, reach, side, core]
        copies = {}
        for offset in offsets:
            slot = reach - offset
            copies[slot] = send(
                own, win.at[p, slot, side, core], zsend.at[p, slot], zrecv.at[p, slot], places[offset]
            )
        ys = {reach: forward(p, reach, side, ysend, yrecv, across)}
        es = {reach: forward(p, reach, side, esend, erecv, twin)}
        return copies, ys, es

    def finish_gather(p, started):
        copies, ys, es = started
        order = [reach] + [reach - offset for offset in reversed(offsets)]
        fs = {}
        lag = 3

        def pass_on(slot):
            ys[slot].wait_recv()
            fs[slot] = forward(p, slot, 1 - side, fsend, frecv, twin)

        for n, slot in enumerate(order):
            if n:
                copies[slot].wait_recv()
                ys[slot] = forward(p, slot, side, ysend, yrecv, across)
                es[slot] = forward(p, slot, side, esend, erecv, twin)
            if n >= lag:
                pass_on(order[n - lag])
        for slot in order[-lag:]:
            pass_on(slot)
        for slot in order:
            es[slot].wait_recv()
        for slot in order:
            fs[slot].wait_recv()
        for slot in order:
            if slot in copies:
                copies[slot].wait_send()
            ys[slot].wait_send()
            es[slot].wait_send()
            fs[slot].wait_send()

    def reduce_blocks(p):
        order = [reach + offset for offset in offsets] + [reach]
        swaps = {}
        for slot in order:
            swaps[slot] = send(acc.at[p, slot, :, 1 - core], got.at[p, slot], asend.at[p, slot], arecv.at[p, slot], twin)
        sides = {}
        for slot in order:
            swaps[slot].wait_recv()
            crossed[p, slot] = acc[p, slot, 1 - side, core] + got[p, slot, 1 - side]
            sides[slot] = send(
                crossed.at[p, slot], crossing.at[p, slot], bsend.at[p, slot], brecv.at[p, slot], across
            )
        copies = {}
        for slot in order:
            sides[slot].wait_recv()
            total = acc[p, slot, side, core] + got[p, slot, side] + crossing[p, slot]
            if slot != reach:
                mixed[p, slot] = total
                copies[slot] = send(
                    mixed.at[p, slot], parts.at[p, slot], rsend.at[p, slot], rrecv.at[p, slot], places[slot - reach]
                )
        for slot in order[:-1]:
            copies[slot].wait_recv()
            total = total + parts[p, slot]
        for slot in order:
            swaps[slot].wait_send()
            sides[slot].wait_send()
            if slot in copies:
                copies[slot].wait_send()
        return total

    def wide(value):
        return jnp.concatenate([value, jnp.zeros((ct, width - value.shape[1]), F32)], axis=1)

    sub = lax.broadcasted_iota(jnp.int32, (slots, LANES), 0)
    lane = lax.broadcasted_iota(jnp.int32, (slots, LANES), 1)
    even = lax.rem(sub, 2) == 0
    low = lane < CAMS
    straight = even == low

    rhs = wide(rhs_ref[0])
    damp = wide(damp_ref[0])
    precond = wide(precond_ref[0])
    vecs[0] = rhs
    scaled = precond * rhs
    bases[0] = scaled
    copies = start_gather(0, scaled)

    shift = layer * (4 * ct)
    spot = lax.broadcasted_iota(jnp.int32, (slots, width), 1)
    spot = jnp.where(spot < rows, spot, spot - rows)
    ids = jnp.concatenate([ids_ref[0] - shift, jnp.zeros((slots, LANES - tiles), jnp.int32)], axis=1)

    def pick_rows(i, carry):
        hots = []
        for u in range(2):
            own = jnp.take_along_axis(ids, jnp.full_like(ids, 2 * i + u), axis=1, mode="promise_in_bounds")
            hots.append(jnp.where(spot == own[:, :1], 1.0, 0.0))
        pick_hot[pl.ds(pl.multiple_of(i * 16, 16), 16), :] = jnp.concatenate(hots, axis=0).astype(BF16)
        return carry

    lax.fori_loop(0, pairs // 16, pick_rows, 0)
    for i in range(pairs // LANES):
        hot = pick_hot[pl.ds(i * LANES, LANES), pl.ds(0, 3 * LANES)].astype(F32)
        hot = jnp.transpose(hot)[:rows].astype(BF16)
        sum_hot[:, pl.ds(i * LANES, LANES)] = hot
        sum_hot[:, pl.ds(pairs + i * LANES, LANES)] = hot
    loads[0].wait()
    loads[1].wait()
    loads[2].wait()
    def live_of(t):
        return sub < counts_ref[0, t]

    def point_rows(t):
        return [pjac[t, r] for r in range(6)]

    camera = lax.broadcasted_iota(jnp.int32, (CAMS, LANES), 0)

    def prepare(i, carry):
        sums = [[] for _ in range(6)]
        for u in range(8):
            t = i * 8 + u
            live = live_of(t)
            p = [jnp.where(live, row, 0.0) for row in point_rows(t)]
            for n, (a, b) in enumerate(((0, 0), (0, 1), (0, 2), (1, 1), (1, 2), (2, 2))):
                sums[n].append(jnp.sum(p[a] * p[b] + p[3 + a] * p[3 + b], axis=0, keepdims=True))
            for k in range(slots):
                index = cidx[t, pl.ds(k, 1), :]
                sel[t, pl.ds(k * CAMS, CAMS), :] = jnp.where(camera == index, 1.0, 0.0).astype(BF16)
        here = pl.ds(pl.multiple_of(i * 8, 8), 8)
        v00, v01, v02, v11, v12, v22 = [jnp.concatenate(part, axis=0) for part in sums]
        v00 = v00 + dpt[0, here, :]
        v11 = v11 + dpt[1, here, :]
        v22 = v22 + dpt[2, here, :]
        c00 = v11 * v22 - v12 * v12
        c01 = v12 * v02 - v01 * v22
        c02 = v01 * v12 - v11 * v02
        c11 = v22 * v00 - v02 * v02
        c12 = v02 * v01 - v00 * v12
        c22 = v00 * v11 - v01 * v01
        det = v00 * c00 + v01 * c01 + v02 * c02
        for n, value in enumerate((c00, c01, c02, c11, c12, c22)):
            inv[n, here, :] = value / det
        return carry

    lax.fori_loop(0, tiles // 8, prepare, 0)
    loads[3].wait()

    def observe(t, u):
        live = live_of(t)
        index = cidx[t]
        above = index + CAMS
        j_rows = [jac[t, r] for r in range(2 * CPAR)]
        p = point_rows(t)
        found = []
        for j in range(CPAR):
            table = picked[pl.ds(t * slots, slots), pl.ds((j // 2) * LANES, LANES)]
            found.append(
                jnp.take_along_axis(table, above if j % 2 else index, axis=1, mode="promise_in_bounds")
            )
        q = []
        for r in range(2):
            total = j_rows[CPAR * r] * found[0]
            for j in range(1, CPAR):
                total = total + j_rows[CPAR * r + j] * found[j]
            q.append(jnp.where(live, total, 0.0))
        y = [jnp.sum(p[a] * q[0] + p[3 + a] * q[1], axis=0, keepdims=True) for a in range(3)]
        m = [inv[n, pl.ds(t, 1), :] for n in range(6)]
        z = [
            m[0] * y[0] + m[1] * y[1] + m[2] * y[2],
            m[1] * y[0] + m[3] * y[1] + m[4] * y[2],
            m[2] * y[0] + m[4] * y[1] + m[5] * y[2],
        ]
        e = []
        for r in range(2):
            back = p[3 * r] * z[0] + p[3 * r + 1] * z[1] + p[3 * r + 2] * z[2]
            e.append(jnp.where(live, q[r] - back, 0.0))
        given = jnp.concatenate([j_rows[j] * e[0] + j_rows[CPAR + j] * e[1] for j in range(CPAR)], axis=0)
        hi, lo = split_two(given)
        given_split[u] = jnp.concatenate([hi, lo], axis=1)
        return q[0] * e[0] + q[1] * e[1]

    def camera_sums(t, u):
        hots = sel[t]
        out = mm(given_split[u], jnp.concatenate([hots, hots], axis=1), NT)

        def diagonal(j):
            block = [out[j * slots : (j + 1) * slots, i * LANES : (i + 1) * LANES] for i in range(slots // 2)]
            value = block[-1]
            for i in range(slots // 2 - 2, -1, -1):
                value = jnp.where(sub < 2 * (i + 1), block[i], value)
            return value

        merged = []
        for i in range(0, CPAR, 2):
            first = diagonal(i)
            second = diagonal(i + 1) if i + 1 < CPAR else jnp.zeros_like(first)
            turned = pltpu.roll(jnp.where(even, second, first), CAMS, 1)
            merged.append(jnp.where(straight, jnp.where(even, first, second), turned))
        return jnp.concatenate(merged, axis=1)

    together = 4
    steps = tiles // together

    def gather_step(i, bend):
        for u in range(together):
            bend = bend + observe(i * together + u, u)
        return bend

    def sum_step(i):
        terms = [camera_sums(i * together + u, u) for u in range(together)]
        for u in range(0, together, 2):
            hi, lo = split_two(jnp.concatenate(terms[u : u + 2], axis=0))
            start = pl.multiple_of((i * together + u) * slots, 16)
            spread[pl.ds(start, 16), :] = hi
            spread[pl.ds(pairs + start, 16), :] = lo

    def both_steps(i, bend):
        sum_step(i - 1)
        return gather_step(i, bend)

    wanted = [(i, j) for j in range(ITERS) for i in range(j + 1)]

    def lane_sums(product):
        line = product[:, :LANES]
        for n in range(1, 5):
            line = line + product[:, n * LANES : (n + 1) * LANES]
        return line

    def start_sums(bend):
        lines = [lane_sums(bases[i] * vecs[j]) for i, j in wanted]
        last = bases[ITERS - 1]
        lines.append(SCALE * (bend + lane_sums(damp * last * last)))
        lines = [jnp.sum(line, axis=0, keepdims=True) for line in lines]
        lines.append(jnp.zeros((8 - len(lines), LANES), F32))
        scal_cam[g] = jnp.concatenate(lines, axis=0)
        return [
            send(scal_cam.at[g], scal_cam.at[g], csend.at[i], crecv.at[i], {"pts": d, "cam": lax.rem(g + i, n_cam)})
            for i in range(1, n_cam)
        ]

    def cross_sums(copies):
        for copy in copies:
            copy.wait()
        total = scal_cam[0]
        for i in range(1, n_cam):
            total = total + scal_cam[i]
        scal_pts[d] = total
        return [
            send(scal_pts.at[d], scal_pts.at[d], osend.at[i], orecv.at[i], {"pts": lax.rem(d + i, n_pts), "cam": g})
            for i in range(1, n_pts)
        ]

    for p in range(ITERS):
        finish_gather(p, copies)
        window = win[p].reshape(rows, width)
        hi, lo = split_two(window)
        win_split[pl.ds(0, rows), :] = hi
        win_split[pl.ds(rows, rows), :] = lo

        def pick(i, carry):
            start = pl.multiple_of(i * LANES, LANES)
            picked[pl.ds(start, LANES), :] = mm(pick_hot[pl.ds(start, LANES), pl.ds(0, 2 * rows)], win_split[...], NN)
            return carry

        lax.fori_loop(0, pairs // LANES, pick, 0)
        bend = gather_step(0, jnp.zeros((slots, LANES), F32))
        bend = lax.fori_loop(1, steps, both_steps, bend)
        sum_step(steps - 1)
        if p + 1 == ITERS:
            started = start_sums(bend)
        for i in range(5):
            cut = pl.ds(i * LANES, LANES)
            value = mm(sum_hot[...], spread[:, cut], NN)
            acc[p, :, :, :, :, cut] = value.reshape(span, 2, 2, ct, LANES)
        if p + 1 == ITERS:
            started = cross_sums(started)
        total = reduce_blocks(p)
        mapped = SCALE * (total + damp * bases[p])
        vecs[p + 1] = mapped
        if p + 1 < ITERS:
            scaled = precond * mapped
            bases[p + 1] = scaled
            copies = start_gather(p + 1, scaled)

    for copy in started:
        copy.wait()
    total = scal_pts[0]
    for i in range(1, n_pts):
        total = total + scal_pts[i]
    sums = jnp.broadcast_to(jnp.sum(total, axis=1, keepdims=True), (8, LANES))
    gram = {}
    for i, (a, b) in enumerate(wanted):
        gram[a, b] = gram[b, a] = sums[i : i + 1, :]
    for i in range(ITERS - 1):
        gram[i, ITERS] = gram[i + 1, ITERS - 1]
    gram[ITERS - 1, ITERS] = sums[len(wanted) : len(wanted) + 1, :]

    one = jnp.ones((1, LANES), F32)
    nil = jnp.zeros((1, LANES), F32)
    x = [nil] * ITERS
    r = [one] + [nil] * ITERS
    s = [one] + [nil] * (ITERS - 1)
    energy = gram[0, 0]
    for p in range(ITERS):
        mapped = [nil] + [value * (1.0 / SCALE) for value in s]
        steep = nil
        for i in range(p + 1):
            row = nil
            for j in range(1, p + 2):
                row = row + mapped[j] * gram[i, j]
            steep = steep + s[i] * row
        step = energy / steep
        x = [a + step * b for a, b in zip(x, s)]
        r = [a - step * b for a, b in zip(r, mapped)]
        if p + 1 < ITERS:
            following = nil
            for i in range(p + 2):
                row = nil
                for j in range(p + 2):
                    row = row + r[j] * gram[i, j]
                following = following + r[i] * row
            ratio = following / energy
            s = [a + ratio * b for a, b in zip(r[:ITERS], s)]
            energy = following

    def spread_out(value):
        return jnp.broadcast_to(value[:, :1], (ct, width))

    solution_value = spread_out(x[0]) * bases[0]
    residual_value = spread_out(r[0]) * vecs[0]
    for i in range(1, ITERS):
        solution_value = solution_value + spread_out(x[i]) * bases[i]
    for i in range(1, ITERS + 1):
        residual_value = residual_value + spread_out(r[i]) * vecs[i]
    sol_ref[0] = solution_value[:, : CPAR * CAMS]
    res_ref[0] = residual_value[:, : CPAR * CAMS]


def solution(mesh):
    n_pts, n_cam = mesh.shape["pts"], mesh.shape["cam"]

    def on_device(rhs, damp_cam, precond, cam_jac, pt_jac, damp_pt, cam_index, tile_ids, counts):
        ct = rhs.shape[1]
        tiles, slots = cam_jac.shape[1:3]
        pairs = tiles * slots
        span = n_pts // 4 + 1
        rows = span * 4 * ct
        width = 5 * LANES
        vmem = pl.BlockSpec(memory_space=pltpu.VMEM)
        anywhere = pl.BlockSpec(memory_space=pl.ANY)
        dma = pltpu.SemaphoreType.DMA
        shape = jax.ShapeDtypeStruct(rhs.shape, F32)
        return pl.pallas_call(
            functools.partial(kernel, n_pts, n_cam, tiles, slots, ct),
            out_shape=(shape, shape),
            in_specs=[vmem] * 4 + [pl.BlockSpec(memory_space=pltpu.SMEM)] + [anywhere] * 4,
            out_specs=(vmem, vmem),
            scratch_shapes=[
                pltpu.VMEM((tiles, 2 * CPAR, slots, LANES), F32),
                pltpu.VMEM((tiles, 6, slots, LANES), F32),
                pltpu.VMEM((3, tiles, LANES), F32),
                pltpu.VMEM((tiles, slots, LANES), jnp.int32),
                pltpu.VMEM((6, tiles, LANES), F32),
                pltpu.VMEM((tiles, slots * CAMS, LANES), BF16),
                pltpu.VMEM((pairs, width), BF16),
                pltpu.VMEM((rows, 2 * pairs), BF16),
                pltpu.VMEM((pairs, width), F32),
                pltpu.VMEM((2 * pairs, width), BF16),
                pltpu.VMEM((2 * rows, width), BF16),
                pltpu.VMEM((4, CPAR * slots, 2 * LANES), BF16),
                pltpu.VMEM((ITERS, span, 2, 2, ct, width), F32),
                pltpu.VMEM((ITERS, span, 2, 2, ct, width), F32),
                pltpu.VMEM((ITERS, span, 2, ct, width), F32),
                pltpu.VMEM((ITERS, span, ct, width), F32),
                pltpu.VMEM((ITERS, span, ct, width), F32),
                pltpu.VMEM((ITERS, span, ct, width), F32),
                pltpu.VMEM((ITERS, span, ct, width), F32),
                pltpu.VMEM((ITERS + 1, ct, width), F32),
                pltpu.VMEM((ITERS, ct, width), F32),
                pltpu.VMEM((n_cam, 8, LANES), F32),
                pltpu.VMEM((n_pts, 8, LANES), F32),
                dma((4,)),
            ]
            + [dma((ITERS, span))] * 14
            + [dma((n_cam,)), dma((n_cam,)), dma((n_pts,)), dma((n_pts,))],
            compiler_params=pltpu.CompilerParams(
                collective_id=0, has_side_effects=True, vmem_limit_bytes=62_000_000
            ),
        )(
            rhs, damp_cam, precond, jnp.swapaxes(tile_ids, 1, 2), counts,
            jnp.swapaxes(cam_jac, 2, 3), jnp.swapaxes(pt_jac, 2, 3), jnp.swapaxes(damp_pt, 1, 2), cam_index,
        )

    return jax.shard_map(
        on_device,
        mesh=mesh,
        in_specs=(
            P("cam", "pts", None),
            P("cam", "pts", None),
            P("cam", "pts", None),
            P("cam", "pts", None, None, None),
            P("cam", "pts", None, None, None),
            P("cam", "pts", None, None),
            P("cam", "pts", None, None),
            P("cam", "pts", None),
            P("cam", "pts"),
        ),
        out_specs=(P("cam", "pts", None), P("cam", "pts", None)),
        check_vma=False,
    )
```

time: 179 us -> 162 us (0.905)
  local copies, waits for them, and re-layouts: 19.3 us -> 2.67 us
    unnamed x6 -> x2, local copies, waits for them, and re-layouts: 17.7 us -> 2.67 us
where the time goes in v2:
time: 162 us
  Pallas kernels  159 us (98%)
  local copies, waits for them, and re-layouts  2.67 us (2%)
    pallas_call x1, Pallas kernels, on_device(): pl.pallas_call(functools.partial(kernel, n_pts, n_cam, tiles, slots, ct),...  159 us

profile of v2, /device:TPU:1, one launch (start us, length us, event | category | flops | bytes accessed | tf_op | source)
XLA Modules:
  0.0 162.2 jit_solution(11812028634727476007)
XLA Ops:
  0.6 158.9 %shard_map.104 = (f32[1,8,576]{2,1,0:T(8,128)}, f32[1,8,576]{2,1,0:T(8,128)}) custom-call(f32[1,8,576]{2,1,0:T(8,128)} %rhs_ref.1, f32[1,8,576]{2,1,0:T(8,128)} %damp_ref.1, f32[1,8,576]{2,1,0:T(8,128)} %precond_ref.1, s32[1,8,96]{2,1,0:T(8,128)} %bitcast.7, s32[1,96]{1,0:T(1,128)} %counts_ref.1, f32[1,96,18,8,128]{4,3,2,1,0:T(8,128)} %bitcast.4, ...), custom_call_target="tpu_custom_call" | custom-call | tf_op jit(solution)/shard_map/pallas_call | solution.py:455
  159.5 1.3 copy.13
  160.9 1.3 copy.14

commit v3 on v2

--- a/solution.py
+++ b/solution.py
@@ -12,6 +12,7 @@
 CAMS = 64
 LANES = 128
 SCALE = 0.125
+TOG = 8
 MESH = pl.DeviceIdType.MESH
 F32 = jnp.float32
 BF16 = jnp.bfloat16
@@ -34,30 +35,28 @@
     cam_jac_ref, pt_jac_ref, damp_pt_ref, cam_index_ref,
     sol_ref, res_ref,
     jac, pjac, dpt, cidx, inv, sel, pick_hot, sum_hot, picked, spread, win_split, given_split,
-    win, acc, got, crossed, crossing, mixed, parts, vecs, bases, scal_cam, scal_pts,
-    in_sem, zsend, zrecv, ysend, yrecv, esend, erecv, fsend, frecv,
-    asend, arecv, bsend, brecv, rsend, rrecv, csend, crecv, osend, orecv,
+    win, acc, got, mixed, parts, vecs, bases, scal_cam, scal_pts,
+    in_sem, wsend, wrecv, fsend, frecv, psend, precv, rsend, rrecv, csend, crecv, osend, orecv,
 ):
-    layers = n_pts // 4
-    quads = layers * n_cam
-    reach = layers // 2
+    half = n_pts // 2
+    chips = half * n_cam
+    reach = half // 2
     span = 2 * reach + 1
-    rows = span * 4 * ct
+    rows = span * 2 * ct
     width = 5 * LANES
+    used = CPAR * CAMS * ct // LANES
     pairs = tiles * slots
     d = lax.axis_index("pts")
     g = lax.axis_index("cam")
-    layer = d // 4
-    side = lax.rem(d, 4) // 2
     core = lax.rem(d, 2)
-    quad = g * layers + layer
+    other = 1 - core
+    chip = g * half + d // 2
 
     def at_offset(offset):
-        place = lax.rem(quad + (offset + quads), quads)
-        return {"pts": lax.rem(place, layers) * 4 + side * 2 + core, "cam": place // layers}
+        place = lax.rem(chip + (offset + chips), chips)
+        return {"pts": lax.rem(place, half) * 2 + core, "cam": place // half}
 
     twin = {"pts": d + 1 - 2 * core, "cam": g}
-    across = {"pts": d + 2 - 4 * side, "cam": g}
     offsets = []
     for far in range(reach, 0, -1):
         offsets += [far, -far]
@@ -85,109 +84,92 @@
         greet({"pts": lax.rem(d + i, n_pts), "cam": g})
     pl.semaphore_wait(barrier, len(offsets) + (n_cam - 1) + (n_pts - 1))
 
+    tail = []
+
     def send(src, dst, ssem, rsem, device):
         copy = pltpu.make_async_remote_copy(
             src_ref=src, dst_ref=dst, send_sem=ssem, recv_sem=rsem, device_id=device, device_id_type=MESH
         )
         copy.start()
+        tail.append(copy)
         return copy
 
-    def forward(p, slot, of_side, ssem, rsem, device):
-        block = win.at[p, slot, of_side, core]
-        return send(block, block, ssem.at[p, slot], rsem.at[p, slot], device)
+    def block(ref, *index):
+        return ref.at[(*index, pl.ds(0, used))]
 
     def start_gather(p, value):
-        win[p, reach, side, core] = value
-        own = win.at[p, reach, side, core]
-        copies = {}
+        win[p, reach, core] = value
+        own = block(win, p, reach, core)
+        copies = []
         for offset in offsets:
             slot = reach - offset
-            copies[slot] = send(
-                own, win.at[p, slot, side, core], zsend.at[p, slot], zrecv.at[p, slot], places[offset]
-            )
-        ys = {reach: forward(p, reach, side, ysend, yrecv, across)}
-        es = {reach: forward(p, reach, side, esend, erecv, twin)}
-        return copies, ys, es
-
-    def finish_gather(p, started):
-        copies, ys, es = started
-        order = [reach] + [reach - offset for offset in reversed(offsets)]
-        fs = {}
-        lag = 3
-
-        def pass_on(slot):
-            ys[slot].wait_recv()
-            fs[slot] = forward(p, slot, 1 - side, fsend, frecv, twin)
-
-        for n, slot in enumerate(order):
-            if n:
-                copies[slot].wait_recv()
-                ys[slot] = forward(p, slot, side, ysend, yrecv, across)
-                es[slot] = forward(p, slot, side, esend, erecv, twin)
-            if n >= lag:
-                pass_on(order[n - lag])
-        for slot in order[-lag:]:
-            pass_on(slot)
-        for slot in order:
-            es[slot].wait_recv()
-        for slot in order:
-            fs[slot].wait_recv()
-        for slot in order:
-            if slot in copies:
-                copies[slot].wait_send()
-            ys[slot].wait_send()
-            es[slot].wait_send()
-            fs[slot].wait_send()
+            copies.append(send(own, block(win, p, slot, core), wsend.at[p, slot], wrecv.at[p, slot], places[offset]))
+        copies.append(send(own, own, fsend.at[p, reach], frecv.at[p, reach], twin))
+        return copies
+
+    def finish_gather(p, copies):
+        forwards = [copies.pop()]
+        for offset, copy in reversed(list(zip(offsets, copies))):
+            copy.wait_recv()
+            slot = reach - offset
+            here = block(win, p, slot, core)
+            forwards.append(send(here, here, fsend.at[p, slot], frecv.at[p, slot], twin))
+        for copy in forwards:
+            copy.wait_recv()
 
     def reduce_blocks(p):
-        order = [reach + offset for offset in offsets] + [reach]
-        swaps = {}
-        for slot in order:
-            swaps[slot] = send(acc.at[p, slot, :, 1 - core], got.at[p, slot], asend.at[p, slot], arecv.at[p, slot], twin)
-        sides = {}
-        for slot in order:
-            swaps[slot].wait_recv()
-            crossed[p, slot] = acc[p, slot, 1 - side, core] + got[p, slot, 1 - side]
-            sides[slot] = send(
-                crossed.at[p, slot], crossing.at[p, slot], bsend.at[p, slot], brecv.at[p, slot], across
-            )
-        copies = {}
-        for slot in order:
-            sides[slot].wait_recv()
-            total = acc[p, slot, side, core] + got[p, slot, side] + crossing[p, slot]
-            if slot != reach:
-                mixed[p, slot] = total
-                copies[slot] = send(
-                    mixed.at[p, slot], parts.at[p, slot], rsend.at[p, slot], rrecv.at[p, slot], places[slot - reach]
+        swaps = []
+        order = offsets + [0]
+        for offset in order:
+            b = reach + offset
+            swaps.append(send(block(acc, p, b, other), block(got, p, b), psend.at[p, b], precv.at[p, b], twin))
+        copies = []
+        for offset, swap in zip(order, swaps):
+            b = reach + offset
+            swap.wait_recv()
+            total = acc[p, b, core] + got[p, b]
+            if offset:
+                mixed[p, b] = total
+                copies.append(
+                    send(block(mixed, p, b), block(parts, p, b), rsend.at[p, b], rrecv.at[p, b], places[offset])
                 )
-        for slot in order[:-1]:
-            copies[slot].wait_recv()
-            total = total + parts[p, slot]
-        for slot in order:
-            swaps[slot].wait_send()
-            sides[slot].wait_send()
-            if slot in copies:
-                copies[slot].wait_send()
-        return total
-
-    def wide(value):
-        return jnp.concatenate([value, jnp.zeros((ct, width - value.shape[1]), F32)], axis=1)
+        for offset, copy in zip(offsets, copies):
+            copy.wait_recv()
+            total = total + parts[p, reach + offset]
+        return jnp.where(filled, total, 0.0)
 
     sub = lax.broadcasted_iota(jnp.int32, (slots, LANES), 0)
     lane = lax.broadcasted_iota(jnp.int32, (slots, LANES), 1)
-    even = lax.rem(sub, 2) == 0
     low = lane < CAMS
-    straight = even == low
-
-    rhs = wide(rhs_ref[0])
-    damp = wide(damp_ref[0])
-    precond = wide(precond_ref[0])
+    early = lax.rem(sub, 4) < 2
+    aligned = early == low
+    top = sub < 4
+    filled = lax.broadcasted_iota(jnp.int32, (5 * ct, LANES), 0) < used
+
+    def pack_last(x):
+        return jnp.where(low, x, pltpu.roll(pltpu.roll(x, 4, 0), CAMS, 1))
+
+    def unpack_last(x):
+        return jnp.where(top, x, pltpu.roll(pltpu.roll(x, 4, 0), CAMS, 1))
+
+    def packed(value):
+        groups = [value[:, n * LANES : (n + 1) * LANES] for n in range(4)]
+        ending = jnp.concatenate([value[:, 4 * LANES :], jnp.zeros((ct, CAMS), F32)], axis=1)
+        return jnp.concatenate(groups + [jnp.where(top, pack_last(ending), 0.0)], axis=0)
+
+    def unpacked(value):
+        groups = [value[n * ct : (n + 1) * ct] for n in range(4)]
+        return jnp.concatenate(groups + [unpack_last(value[4 * ct :])[:, :CAMS]], axis=1)
+
+    rhs = packed(rhs_ref[0])
+    damp = packed(damp_ref[0])
+    precond = packed(precond_ref[0])
     vecs[0] = rhs
     scaled = precond * rhs
     bases[0] = scaled
     copies = start_gather(0, scaled)
 
-    shift = layer * (4 * ct)
+    shift = (d // 2) * (2 * ct)
     spot = lax.broadcasted_iota(jnp.int32, (slots, width), 1)
     spot = jnp.where(spot < rows, spot, spot - rows)
     ids = jnp.concatenate([ids_ref[0] - shift, jnp.zeros((slots, LANES - tiles), jnp.int32)], axis=1)
@@ -227,7 +209,8 @@
                 sums[n].append(jnp.sum(p[a] * p[b] + p[3 + a] * p[3 + b], axis=0, keepdims=True))
             for k in range(slots):
                 index = cidx[t, pl.ds(k, 1), :]
-                sel[t, pl.ds(k * CAMS, CAMS), :] = jnp.where(camera == index, 1.0, 0.0).astype(BF16)
+                hot = jnp.where(camera == index, 1.0, 0.0).astype(BF16)
+                sel[t, pl.ds((k // 2) * CAMS, CAMS), pl.ds((k % 2) * LANES, LANES)] = hot
         here = pl.ds(pl.multiple_of(i * 8, 8), 8)
         v00, v01, v02, v11, v12, v22 = [jnp.concatenate(part, axis=0) for part in sums]
         v00 = v00 + dpt[0, here, :]
@@ -246,6 +229,15 @@
 
     lax.fori_loop(0, tiles // 8, prepare, 0)
     loads[3].wait()
+
+    together = TOG
+    lower = 80
+    parity = lax.rem(lax.broadcasted_iota(jnp.int32, (CPAR * slots, LANES), 0), 2)
+    odd_rows = parity.astype(F32).astype(BF16)
+    even_rows = (1 - parity).astype(F32).astype(BF16)
+    for u in range(together):
+        given_split[u, pl.ds(64, 16), :] = jnp.zeros((16, 2 * LANES), BF16)
+        given_split[u, pl.ds(lower + 64, 16), :] = jnp.zeros((16, 2 * LANES), BF16)
 
     def observe(t, u):
         live = live_of(t)
@@ -278,29 +270,31 @@
             e.append(jnp.where(live, q[r] - back, 0.0))
         given = jnp.concatenate([j_rows[j] * e[0] + j_rows[CPAR + j] * e[1] for j in range(CPAR)], axis=0)
         hi, lo = split_two(given)
-        given_split[u] = jnp.concatenate([hi, lo], axis=1)
+        heights = CPAR * slots
+        given_split[u, pl.ds(0, heights), :] = jnp.concatenate([hi * even_rows, hi * odd_rows], axis=1)
+        given_split[u, pl.ds(lower, heights), :] = jnp.concatenate([lo * even_rows, lo * odd_rows], axis=1)
         return q[0] * e[0] + q[1] * e[1]
 
     def camera_sums(t, u):
-        hots = sel[t]
-        out = mm(given_split[u], jnp.concatenate([hots, hots], axis=1), NT)
+        out = mm(given_split[u], sel[t], NT)
 
         def diagonal(j):
-            block = [out[j * slots : (j + 1) * slots, i * LANES : (i + 1) * LANES] for i in range(slots // 2)]
-            value = block[-1]
-            for i in range(slots // 2 - 2, -1, -1):
-                value = jnp.where(sub < 2 * (i + 1), block[i], value)
-            return value
+            both = []
+            for n in range(slots // 4):
+                cut = slice(n * LANES, (n + 1) * LANES)
+                both.append(
+                    out[j * slots : (j + 1) * slots, cut] + out[lower + j * slots : lower + (j + 1) * slots, cut]
+                )
+            return jnp.where(top, both[0], both[1])
 
         merged = []
         for i in range(0, CPAR, 2):
             first = diagonal(i)
             second = diagonal(i + 1) if i + 1 < CPAR else jnp.zeros_like(first)
-            turned = pltpu.roll(jnp.where(even, second, first), CAMS, 1)
-            merged.append(jnp.where(straight, jnp.where(even, first, second), turned))
+            turned = pltpu.roll(jnp.where(early, second, first), CAMS, 1)
+            merged.append(jnp.where(aligned, jnp.where(early, first, second), turned))
         return jnp.concatenate(merged, axis=1)
 
-    together = 4
     steps = tiles // together
 
     def gather_step(i, bend):
@@ -323,9 +317,9 @@
     wanted = [(i, j) for j in range(ITERS) for i in range(j + 1)]
 
     def lane_sums(product):
-        line = product[:, :LANES]
+        line = product[:ct]
         for n in range(1, 5):
-            line = line + product[:, n * LANES : (n + 1) * LANES]
+            line = line + product[n * ct : (n + 1) * ct]
         return line
 
     def start_sums(bend):
@@ -342,7 +336,7 @@
 
     def cross_sums(copies):
         for copy in copies:
-            copy.wait()
+            copy.wait_recv()
         total = scal_cam[0]
         for i in range(1, n_cam):
             total = total + scal_cam[i]
@@ -354,10 +348,16 @@
 
     for p in range(ITERS):
         finish_gather(p, copies)
-        window = win[p].reshape(rows, width)
-        hi, lo = split_two(window)
-        win_split[pl.ds(0, rows), :] = hi
-        win_split[pl.ds(rows, rows), :] = lo
+        for n in range(5):
+            window = win[p, :, :, pl.ds(n * ct, ct), :].reshape(rows, LANES)
+            if n == 4:
+                window = jnp.concatenate(
+                    [unpack_last(window[i * ct : (i + 1) * ct]) for i in range(2 * span)], axis=0
+                )
+            hi, lo = split_two(window)
+            cut = pl.ds(n * LANES, LANES)
+            win_split[pl.ds(0, rows), cut] = hi
+            win_split[pl.ds(rows, rows), cut] = lo
 
         def pick(i, carry):
             start = pl.multiple_of(i * LANES, LANES)
@@ -373,7 +373,9 @@
         for i in range(5):
             cut = pl.ds(i * LANES, LANES)
             value = mm(sum_hot[...], spread[:, cut], NN)
-            acc[p, :, :, :, :, cut] = value.reshape(span, 2, 2, ct, LANES)
+            if i == 4:
+                value = jnp.concatenate([pack_last(value[n * ct : (n + 1) * ct]) for n in range(2 * span)], axis=0)
+            acc[p, :, :, pl.ds(i * ct, ct), :] = value.reshape(span, 2, ct, LANES)
         if p + 1 == ITERS:
             started = cross_sums(started)
         total = reduce_blocks(p)
@@ -385,7 +387,7 @@
             copies = start_gather(p + 1, scaled)
 
     for copy in started:
-        copy.wait()
+        copy.wait_recv()
     total = scal_pts[0]
     for i in range(1, n_pts):
         total = total + scal_pts[i]
@@ -426,7 +428,7 @@
             energy = following
 
     def spread_out(value):
-        return jnp.broadcast_to(value[:, :1], (ct, width))
+        return jnp.broadcast_to(value, (5 * ct, LANES))
 
     solution_value = spread_out(x[0]) * bases[0]
     residual_value = spread_out(r[0]) * vecs[0]
@@ -434,8 +436,10 @@
         solution_value = solution_value + spread_out(x[i]) * bases[i]
     for i in range(1, ITERS + 1):
         residual_value = residual_value + spread_out(r[i]) * vecs[i]
-    sol_ref[0] = solution_value[:, : CPAR * CAMS]
-    res_ref[0] = residual_value[:, : CPAR * CAMS]
+    for copy in tail:
+        copy.wait_send()
+    sol_ref[0] = unpacked(solution_value)
+    res_ref[0] = unpacked(residual_value)
 
 
 def solution(mesh):
@@ -445,8 +449,8 @@
         ct = rhs.shape[1]
         tiles, slots = cam_jac.shape[1:3]
         pairs = tiles * slots
-        span = n_pts // 4 + 1
-        rows = span * 4 * ct
+        span = n_pts // 2 + 1
+        rows = span * 2 * ct
         width = 5 * LANES
         vmem = pl.BlockSpec(memory_space=pltpu.VMEM)
         anywhere = pl.BlockSpec(memory_space=pl.ANY)
@@ -463,27 +467,25 @@
                 pltpu.VMEM((3, tiles, LANES), F32),
                 pltpu.VMEM((tiles, slots, LANES), jnp.int32),
                 pltpu.VMEM((6, tiles, LANES), F32),
-                pltpu.VMEM((tiles, slots * CAMS, LANES), BF16),
+                pltpu.VMEM((tiles, slots * CAMS // 2, 2 * LANES), BF16),
                 pltpu.VMEM((pairs, width), BF16),
                 pltpu.VMEM((rows, 2 * pairs), BF16),
                 pltpu.VMEM((pairs, width), F32),
                 pltpu.VMEM((2 * pairs, width), BF16),
                 pltpu.VMEM((2 * rows, width), BF16),
-                pltpu.VMEM((4, CPAR * slots, 2 * LANES), BF16),
-                pltpu.VMEM((ITERS, span, 2, 2, ct, width), F32),
-                pltpu.VMEM((ITERS, span, 2, 2, ct, width), F32),
-                pltpu.VMEM((ITERS, span, 2, ct, width), F32),
-                pltpu.VMEM((ITERS, span, ct, width), F32),
-                pltpu.VMEM((ITERS, span, ct, width), F32),
-                pltpu.VMEM((ITERS, span, ct, width), F32),
-                pltpu.VMEM((ITERS, span, ct, width), F32),
-                pltpu.VMEM((ITERS + 1, ct, width), F32),
-                pltpu.VMEM((ITERS, ct, width), F32),
+                pltpu.VMEM((TOG, 160, 2 * LANES), BF16),
+                pltpu.VMEM((ITERS, span, 2, 5 * ct, LANES), F32),
+                pltpu.VMEM((ITERS, span, 2, 5 * ct, LANES), F32),
+                pltpu.VMEM((ITERS, span, 5 * ct, LANES), F32),
+                pltpu.VMEM((ITERS, span, 5 * ct, LANES), F32),
+                pltpu.VMEM((ITERS, span, 5 * ct, LANES), F32),
+                pltpu.VMEM((ITERS + 1, 5 * ct, LANES), F32),
+                pltpu.VMEM((ITERS, 5 * ct, LANES), F32),
                 pltpu.VMEM((n_cam, 8, LANES), F32),
                 pltpu.VMEM((n_pts, 8, LANES), F32),
                 dma((4,)),
             ]
-            + [dma((ITERS, span))] * 14
+            + [dma((ITERS, span))] * 8
             + [dma((n_cam,)), dma((n_cam,)), dma((n_pts,)), dma((n_pts,))],
             compiler_params=pltpu.CompilerParams(
                 collective_id=0, has_side_effects=True, vmem_limit_bytes=62_000_000

time: 162 us -> 132 us (0.81)
  Pallas kernels: 159 us -> 129 us
    pallas_call x1, Pallas kernels: 159 us -> 129 us  [on_device(): pl.pallas_call(functools.partial(kernel, n_pts, n_cam, tiles, slots, ct),...]
where the time goes in v3:
time: 132 us
  Pallas kernels  129 us (98%)
  local copies, waits for them, and re-layouts  2.67 us (2%)
    pallas_call x1, Pallas kernels, on_device(): pl.pallas_call(functools.partial(kernel, n_pts, n_cam, tiles, slots, ct),...  129 us
    unnamed x2, local copies, waits for them, and re-layouts  2.67 us

profile of v3, /device:TPU:1, one launch (start us, length us, event | category | flops | bytes accessed | tf_op | source)
XLA Modules:
  0.0 132.2 jit_solution(7206224759274990370)
XLA Ops:
  0.6 128.9 %shard_map.104 = (f32[1,8,576]{2,1,0:T(8,128)}, f32[1,8,576]{2,1,0:T(8,128)}) custom-call(f32[1,8,576]{2,1,0:T(8,128)} %rhs_ref.1, f32[1,8,576]{2,1,0:T(8,128)} %damp_ref.1, f32[1,8,576]{2,1,0:T(8,128)} %precond_ref.1, s32[1,8,96]{2,1,0:T(8,128)} %bitcast.7, s32[1,96]{1,0:T(1,128)} %counts_ref.1, f32[1,96,18,8,128]{4,3,2,1,0:T(8,128)} %bitcast.4, ...), custom_call_target="tpu_custom_call" | custom-call | tf_op jit(solution)/shard_map/pallas_call | solution.py:459
  129.6 1.3 %copy.13 = f32[1,8,576]{2,1,0:T(8,128)} copy(f32[1,8,576]{2,1,0:T(8,128)} %get-tuple-element.4) | data formatting | bytes 36864
  130.9 1.3 %copy.14 = f32[1,8,576]{2,1,0:T(8,128)} copy(f32[1,8,576]{2,1,0:T(8,128)} %get-tuple-element.5) | data formatting | bytes 36864

commit v4 on v3

--- a/solution.py
+++ b/solution.py
@@ -12,7 +12,7 @@
 CAMS = 64
 LANES = 128
 SCALE = 0.125
-TOG = 8
+TOG = 12
 MESH = pl.DeviceIdType.MESH
 F32 = jnp.float32
 BF16 = jnp.bfloat16
@@ -34,7 +34,7 @@
     rhs_ref, damp_ref, precond_ref, ids_ref, counts_ref,
     cam_jac_ref, pt_jac_ref, damp_pt_ref, cam_index_ref,
     sol_ref, res_ref,
-    jac, pjac, dpt, cidx, inv, sel, pick_hot, sum_hot, picked, spread, win_split, given_split,
+    jac, pjac, dpt, cidx, inv, sel, pick_hot, sum_hot, picked, spread, win_split, found, given_split,
     win, acc, got, mixed, parts, vecs, bases, scal_cam, scal_pts,
     in_sem, wsend, wrecv, fsend, frecv, psend, precv, rsend, rrecv, csend, crecv, osend, orecv,
 ):
@@ -65,7 +65,7 @@
     loads = [
         pltpu.make_async_copy(pt_jac_ref.at[0], pjac, in_sem.at[0]),
         pltpu.make_async_copy(damp_pt_ref.at[0], dpt, in_sem.at[1]),
-        pltpu.make_async_copy(cam_index_ref.at[0], cidx, in_sem.at[2]),
+        pltpu.make_async_copy(cam_index_ref.at[0], cidx.at[pl.ds(0, tiles)], in_sem.at[2]),
         pltpu.make_async_copy(cam_jac_ref.at[0], jac, in_sem.at[3]),
     ]
     for load in loads:
@@ -93,6 +93,12 @@
         copy.start()
         tail.append(copy)
         return copy
+
+    def drain(keep):
+        waiting = [copy for copy in tail if all(copy is not kept for kept in keep)]
+        tail[:] = keep
+        for copy in waiting:
+            copy.wait_send()
 
     def block(ref, *index):
         return ref.at[(*index, pl.ds(0, used))]
@@ -109,6 +115,7 @@
 
     def finish_gather(p, copies):
         forwards = [copies.pop()]
+        drain(copies + forwards)
         for offset, copy in reversed(list(zip(offsets, copies))):
             copy.wait_recv()
             slot = reach - offset
@@ -117,12 +124,13 @@
         for copy in forwards:
             copy.wait_recv()
 
-    def reduce_blocks(p):
+    def reduce_blocks(p, keep):
         swaps = []
         order = offsets + [0]
         for offset in order:
             b = reach + offset
             swaps.append(send(block(acc, p, b, other), block(got, p, b), psend.at[p, b], precv.at[p, b], twin))
+        drain(swaps + keep)
         copies = []
         for offset, swap in zip(order, swaps):
             b = reach + offset
@@ -191,6 +199,7 @@
     loads[0].wait()
     loads[1].wait()
     loads[2].wait()
+    loads[3].wait()
     def live_of(t):
         return sub < counts_ref[0, t]
 
@@ -205,12 +214,14 @@
             t = i * 8 + u
             live = live_of(t)
             p = [jnp.where(live, row, 0.0) for row in point_rows(t)]
+            for r in range(2 * CPAR):
+                jac[t, r] = jnp.where(live, jac[t, r], 0.0)
             for n, (a, b) in enumerate(((0, 0), (0, 1), (0, 2), (1, 1), (1, 2), (2, 2))):
                 sums[n].append(jnp.sum(p[a] * p[b] + p[3 + a] * p[3 + b], axis=0, keepdims=True))
             for k in range(slots):
                 index = cidx[t, pl.ds(k, 1), :]
                 hot = jnp.where(camera == index, 1.0, 0.0).astype(BF16)
-                sel[t, pl.ds((k // 2) * CAMS, CAMS), pl.ds((k % 2) * LANES, LANES)] = hot
+                sel[TOG + t, pl.ds((k // 2) * CAMS, CAMS), pl.ds((k % 2) * LANES, LANES)] = hot
         here = pl.ds(pl.multiple_of(i * 8, 8), 8)
         v00, v01, v02, v11, v12, v22 = [jnp.concatenate(part, axis=0) for part in sums]
         v00 = v00 + dpt[0, here, :]
@@ -228,7 +239,6 @@
         return carry
 
     lax.fori_loop(0, tiles // 8, prepare, 0)
-    loads[3].wait()
 
     together = TOG
     lower = 80
@@ -236,27 +246,25 @@
     odd_rows = parity.astype(F32).astype(BF16)
     even_rows = (1 - parity).astype(F32).astype(BF16)
     for u in range(together):
-        given_split[u, pl.ds(64, 16), :] = jnp.zeros((16, 2 * LANES), BF16)
-        given_split[u, pl.ds(lower + 64, 16), :] = jnp.zeros((16, 2 * LANES), BF16)
+        cidx[tiles + u] = jnp.zeros((slots, LANES), jnp.int32)
+        given_split[u] = jnp.zeros((2 * lower, 2 * LANES), BF16)
+
+    def look_up(t, u):
+        index = cidx[t]
+        for first in range(2):
+            for j in range(first, CPAR, 2):
+                table = picked[pl.ds(t * slots, slots), pl.ds((j // 2) * LANES, LANES)]
+                found[u, j] = jnp.take_along_axis(table, index + CAMS * first, axis=1, mode="promise_in_bounds")
 
     def observe(t, u):
-        live = live_of(t)
-        index = cidx[t]
-        above = index + CAMS
         j_rows = [jac[t, r] for r in range(2 * CPAR)]
         p = point_rows(t)
-        found = []
-        for j in range(CPAR):
-            table = picked[pl.ds(t * slots, slots), pl.ds((j // 2) * LANES, LANES)]
-            found.append(
-                jnp.take_along_axis(table, above if j % 2 else index, axis=1, mode="promise_in_bounds")
-            )
         q = []
         for r in range(2):
-            total = j_rows[CPAR * r] * found[0]
+            total = j_rows[CPAR * r] * found[u, 0]
             for j in range(1, CPAR):
-                total = total + j_rows[CPAR * r + j] * found[j]
-            q.append(jnp.where(live, total, 0.0))
+                total = total + j_rows[CPAR * r + j] * found[u, j]
+            q.append(total)
         y = [jnp.sum(p[a] * q[0] + p[3 + a] * q[1], axis=0, keepdims=True) for a in range(3)]
         m = [inv[n, pl.ds(t, 1), :] for n in range(6)]
         z = [
@@ -267,7 +275,7 @@
         e = []
         for r in range(2):
             back = p[3 * r] * z[0] + p[3 * r + 1] * z[1] + p[3 * r + 2] * z[2]
-            e.append(jnp.where(live, q[r] - back, 0.0))
+            e.append(q[r] - back)
         given = jnp.concatenate([j_rows[j] * e[0] + j_rows[CPAR + j] * e[1] for j in range(CPAR)], axis=0)
         hi, lo = split_two(given)
         heights = CPAR * slots
@@ -297,7 +305,11 @@
 
     steps = tiles // together
 
-    def gather_step(i, bend):
+    def look_step(i):
+        for u in range(together):
+            look_up(i * together + u, u)
+
+    def observe_step(i, bend):
         for u in range(together):
             bend = bend + observe(i * together + u, u)
         return bend
@@ -307,12 +319,14 @@
         for u in range(0, together, 2):
             hi, lo = split_two(jnp.concatenate(terms[u : u + 2], axis=0))
             start = pl.multiple_of((i * together + u) * slots, 16)
-            spread[pl.ds(start, 16), :] = hi
-            spread[pl.ds(pairs + start, 16), :] = lo
-
-    def both_steps(i, bend):
-        sum_step(i - 1)
-        return gather_step(i, bend)
+            spread[0, pl.ds(start, 16), :] = hi
+            spread[1, pl.ds(start, 16), :] = lo
+
+    def all_steps(i, bend):
+        sum_step(i)
+        bend = observe_step(i, bend)
+        look_step(i + 1)
+        return bend
 
     wanted = [(i, j) for j in range(ITERS) for i in range(j + 1)]
 
@@ -360,25 +374,30 @@
             win_split[pl.ds(rows, rows), cut] = lo
 
         def pick(i, carry):
-            start = pl.multiple_of(i * LANES, LANES)
-            picked[pl.ds(start, LANES), :] = mm(pick_hot[pl.ds(start, LANES), pl.ds(0, 2 * rows)], win_split[...], NN)
+            here = pl.ds(pl.multiple_of(i * (pairs // 2), 16), pairs // 2)
+            picked[here, :] = mm(pick_hot[here, pl.ds(0, 2 * rows)], win_split[...], NN)
             return carry
 
-        lax.fori_loop(0, pairs // LANES, pick, 0)
-        bend = gather_step(0, jnp.zeros((slots, LANES), F32))
-        bend = lax.fori_loop(1, steps, both_steps, bend)
-        sum_step(steps - 1)
+        lax.fori_loop(0, 2, pick, 0)
+        look_step(0)
+        bend = lax.fori_loop(0, steps, all_steps, jnp.zeros((slots, LANES), F32))
+        sum_step(steps)
         if p + 1 == ITERS:
             started = start_sums(bend)
-        for i in range(5):
-            cut = pl.ds(i * LANES, LANES)
-            value = mm(sum_hot[...], spread[:, cut], NN)
-            if i == 4:
-                value = jnp.concatenate([pack_last(value[n * ct : (n + 1) * ct]) for n in range(2 * span)], axis=0)
-            acc[p, :, :, pl.ds(i * ct, ct), :] = value.reshape(span, 2, ct, LANES)
+        for low_group, high_group in ((0, 2), (2, 4), (4, 5)):
+            cut = pl.ds(low_group * LANES, (high_group - low_group) * LANES)
+            given = jnp.concatenate([spread[n, pl.ds(TOG * slots, pairs), cut] for n in range(2)], axis=0)
+            sums = mm(sum_hot[...], given, NN)
+            for i in range(low_group, high_group):
+                value = sums[:, (i - low_group) * LANES : (i - low_group + 1) * LANES]
+                if i == 4:
+                    value = jnp.concatenate(
+                        [pack_last(value[n * ct : (n + 1) * ct]) for n in range(2 * span)], axis=0
+                    )
+                acc[p, :, :, pl.ds(i * ct, ct), :] = value.reshape(span, 2, ct, LANES)
         if p + 1 == ITERS:
             started = cross_sums(started)
-        total = reduce_blocks(p)
+        total = reduce_blocks(p, started if p + 1 == ITERS else [])
         mapped = SCALE * (total + damp * bases[p])
         vecs[p + 1] = mapped
         if p + 1 < ITERS:
@@ -436,8 +455,7 @@
         solution_value = solution_value + spread_out(x[i]) * bases[i]
     for i in range(1, ITERS + 1):
         residual_value = residual_value + spread_out(r[i]) * vecs[i]
-    for copy in tail:
-        copy.wait_send()
+    drain([])
     sol_ref[0] = unpacked(solution_value)
     res_ref[0] = unpacked(residual_value)
 
@@ -465,14 +483,15 @@
                 pltpu.VMEM((tiles, 2 * CPAR, slots, LANES), F32),
                 pltpu.VMEM((tiles, 6, slots, LANES), F32),
                 pltpu.VMEM((3, tiles, LANES), F32),
-                pltpu.VMEM((tiles, slots, LANES), jnp.int32),
+                pltpu.VMEM((tiles + TOG, slots, LANES), jnp.int32),
                 pltpu.VMEM((6, tiles, LANES), F32),
-                pltpu.VMEM((tiles, slots * CAMS // 2, 2 * LANES), BF16),
+                pltpu.VMEM((TOG + tiles, slots * CAMS // 2, 2 * LANES), BF16),
                 pltpu.VMEM((pairs, width), BF16),
                 pltpu.VMEM((rows, 2 * pairs), BF16),
-                pltpu.VMEM((pairs, width), F32),
-                pltpu.VMEM((2 * pairs, width), BF16),
+                pltpu.VMEM((pairs + TOG * slots, width), F32),
+                pltpu.VMEM((2, TOG * slots + pairs, width), BF16),
                 pltpu.VMEM((2 * rows, width), BF16),
+                pltpu.VMEM((TOG, CPAR, slots, LANES), F32),
                 pltpu.VMEM((TOG, 160, 2 * LANES), BF16),
                 pltpu.VMEM((ITERS, span, 2, 5 * ct, LANES), F32),
                 pltpu.VMEM((ITERS, span, 2, 5 * ct, LANES), F32),

time: 132 us -> 127 us (0.962)
  Pallas kernels: 129 us -> 123 us
    pallas_call x1, Pallas kernels: 129 us -> 123 us  [on_device(): pl.pallas_call(functools.partial(kernel, n_pts, n_cam, tiles, slots, ct),...]
where the time goes in v4:
time: 127 us
  Pallas kernels  123 us (97%)
  local copies, waits for them, and re-layouts  2.67 us (2%)
    pallas_call x1, Pallas kernels, on_device(): pl.pallas_call(functools.partial(kernel, n_pts, n_cam, tiles, slots, ct),...  123 us
    unnamed x2, local copies, waits for them, and re-layouts  2.67 us

profile of v4, /device:TPU:1, one launch (start us, length us, event | category | flops | bytes accessed | tf_op | source)
XLA Modules:
  0.0 126.7 jit_solution(11635097177291707128)
XLA Ops:
  0.6 123.4 %shard_map.104 = (f32[1,8,576]{2,1,0:T(8,128)}, f32[1,8,576]{2,1,0:T(8,128)}) custom-call(f32[1,8,576]{2,1,0:T(8,128)} %rhs_ref.1, f32[1,8,576]{2,1,0:T(8,128)} %damp_ref.1, f32[1,8,576]{2,1,0:T(8,128)} %precond_ref.1, s32[1,8,96]{2,1,0:T(8,128)} %bitcast.7, s32[1,96]{1,0:T(1,128)} %counts_ref.1, f32[1,96,18,8,128]{4,3,2,1,0:T(8,128)} %bitcast.4, ...), custom_call_target="tpu_custom_call" | custom-call | tf_op jit(solution)/shard_map/pallas_call | solution.py:477
  124.0 1.3 %copy.13 = f32[1,8,576]{2,1,0:T(8,128)} copy(f32[1,8,576]{2,1,0:T(8,128)} %get-tuple-element.4) | data formatting | bytes 36864
  125.3 1.3 %copy.14 = f32[1,8,576]{2,1,0:T(8,128)} copy(f32[1,8,576]{2,1,0:T(8,128)} %get-tuple-element.5) | data formatting | bytes 36864

commit v5 on v4

--- a/solution.py
+++ b/solution.py
@@ -33,7 +33,7 @@
     n_pts, n_cam, tiles, slots, ct,
     rhs_ref, damp_ref, precond_ref, ids_ref, counts_ref,
     cam_jac_ref, pt_jac_ref, damp_pt_ref, cam_index_ref,
-    sol_ref, res_ref,
+    out_ref,
     jac, pjac, dpt, cidx, inv, sel, pick_hot, sum_hot, picked, spread, win_split, found, given_split,
     win, acc, got, mixed, parts, vecs, bases, scal_cam, scal_pts,
     in_sem, wsend, wrecv, fsend, frecv, psend, precv, rsend, rrecv, csend, crecv, osend, orecv,
@@ -82,7 +82,6 @@
         greet({"pts": d, "cam": lax.rem(g + i, n_cam)})
     for i in range(1, n_pts):
         greet({"pts": lax.rem(d + i, n_pts), "cam": g})
-    pl.semaphore_wait(barrier, len(offsets) + (n_cam - 1) + (n_pts - 1))
 
     tail = []
 
@@ -116,7 +115,7 @@
     def finish_gather(p, copies):
         forwards = [copies.pop()]
         drain(copies + forwards)
-        for offset, copy in reversed(list(zip(offsets, copies))):
+        for offset, copy in list(zip(offsets, copies)):
             copy.wait_recv()
             slot = reach - offset
             here = block(win, p, slot, core)
@@ -124,7 +123,7 @@
         for copy in forwards:
             copy.wait_recv()
 
-    def reduce_blocks(p, keep):
+    def reduce_blocks(p, keep, meanwhile):
         swaps = []
         order = offsets + [0]
         for offset in order:
@@ -141,6 +140,7 @@
                 copies.append(
                     send(block(mixed, p, b), block(parts, p, b), rsend.at[p, b], rrecv.at[p, b], places[offset])
                 )
+        meanwhile()
         for offset, copy in zip(offsets, copies):
             copy.wait_recv()
             total = total + parts[p, reach + offset]
@@ -172,11 +172,6 @@
     rhs = packed(rhs_ref[0])
     damp = packed(damp_ref[0])
     precond = packed(precond_ref[0])
-    vecs[0] = rhs
-    scaled = precond * rhs
-    bases[0] = scaled
-    copies = start_gather(0, scaled)
-
     shift = (d // 2) * (2 * ct)
     spot = lax.broadcasted_iota(jnp.int32, (slots, width), 1)
     spot = jnp.where(spot < rows, spot, spot - rows)
@@ -196,6 +191,12 @@
         hot = jnp.transpose(hot)[:rows].astype(BF16)
         sum_hot[:, pl.ds(i * LANES, LANES)] = hot
         sum_hot[:, pl.ds(pairs + i * LANES, LANES)] = hot
+    pl.semaphore_wait(barrier, len(offsets) + (n_cam - 1) + (n_pts - 1))
+    vecs[0] = rhs
+    scaled = precond * rhs
+    bases[0] = scaled
+    copies = start_gather(0, scaled)
+
     loads[0].wait()
     loads[1].wait()
     loads[2].wait()
@@ -395,9 +396,13 @@
                         [pack_last(value[n * ct : (n + 1) * ct]) for n in range(2 * span)], axis=0
                     )
                 acc[p, :, :, pl.ds(i * ct, ct), :] = value.reshape(span, 2, ct, LANES)
-        if p + 1 == ITERS:
-            started = cross_sums(started)
-        total = reduce_blocks(p, started if p + 1 == ITERS else [])
+        crossing = []
+
+        def meanwhile():
+            if p + 1 == ITERS:
+                crossing.extend(cross_sums(started))
+
+        total = reduce_blocks(p, started if p + 1 == ITERS else [], meanwhile)
         mapped = SCALE * (total + damp * bases[p])
         vecs[p + 1] = mapped
         if p + 1 < ITERS:
@@ -405,7 +410,7 @@
             bases[p + 1] = scaled
             copies = start_gather(p + 1, scaled)
 
-    for copy in started:
+    for copy in crossing:
         copy.wait_recv()
     total = scal_pts[0]
     for i in range(1, n_pts):
@@ -456,8 +461,8 @@
     for i in range(1, ITERS + 1):
         residual_value = residual_value + spread_out(r[i]) * vecs[i]
     drain([])
-    sol_ref[0] = unpacked(solution_value)
-    res_ref[0] = unpacked(residual_value)
+    out_ref[0] = unpacked(solution_value)
+    out_ref[1] = unpacked(residual_value)
 
 
 def solution(mesh):
@@ -473,12 +478,11 @@
         vmem = pl.BlockSpec(memory_space=pltpu.VMEM)
         anywhere = pl.BlockSpec(memory_space=pl.ANY)
         dma = pltpu.SemaphoreType.DMA
-        shape = jax.ShapeDtypeStruct(rhs.shape, F32)
-        return pl.pallas_call(
+        both = pl.pallas_call(
             functools.partial(kernel, n_pts, n_cam, tiles, slots, ct),
-            out_shape=(shape, shape),
+            out_shape=jax.ShapeDtypeStruct((2, *rhs.shape[1:]), F32),
             in_specs=[vmem] * 4 + [pl.BlockSpec(memory_space=pltpu.SMEM)] + [anywhere] * 4,
-            out_specs=(vmem, vmem),
+            out_specs=vmem,
             scratch_shapes=[
                 pltpu.VMEM((tiles, 2 * CPAR, slots, LANES), F32),
                 pltpu.VMEM((tiles, 6, slots, LANES), F32),
@@ -513,6 +517,7 @@
             rhs, damp_cam, precond, jnp.swapaxes(tile_ids, 1, 2), counts,
             jnp.swapaxes(cam_jac, 2, 3), jnp.swapaxes(pt_jac, 2, 3), jnp.swapaxes(damp_pt, 1, 2), cam_index,
         )
+        return both[:1], both[1:]
 
     return jax.shard_map(
         on_device,

time: 127 us -> 126 us (level)
  local copies, waits for them, and re-layouts: 2.67 us -> 1.36 us
    unnamed x2 -> x0, local copies, waits for them, and re-layouts: 2.67 us -> none
    slice x0 -> x1, local copies, waits for them, and re-layouts: none -> 1.36 us  [on_device(): return (both[:1], both[1:])]
where the time goes in v5:
time: 126 us; the launch traced here: 125 us
  Pallas kernels  123 us (98%)
  local copies, waits for them, and re-layouts  1.36 us (1%)
    pallas_call x1, Pallas kernels, on_device(): pl.pallas_call(functools.partial(kernel, n_pts, n_cam, tiles, slots, ct),...  123 us

profile of v5, /device:TPU:1, one launch (start us, length us, event | category | flops | bytes accessed | tf_op | source)
XLA Modules:
  0.0 125.4 jit_solution(12114325710526662302)
XLA Ops:
  0.6 123.4 %shard_map.104 = f32[2,8,576]{2,1,0:T(8,128)} custom-call(f32[1,8,576]{2,1,0:T(8,128)} %rhs_ref.1, f32[1,8,576]{2,1,0:T(8,128)} %damp_ref.1, f32[1,8,576]{2,1,0:T(8,128)} %precond_ref.1, s32[1,8,96]{2,1,0:T(8,128)} %bitcast.7, s32[1,96]{1,0:T(1,128)} %counts_ref.1, f32[1,96,18,8,128]{4,3,2,1,0:T(8,128)} %bitcast.4, f32[1,96,6,8,128]{4,3,2,1,0:T(8,128)} %bitcast.5, ...), custom_call_target="tpu_custom_call" | custom-call | tf_op jit(solution)/shard_map/pallas_call | solution.py:481
  124.1 1.4 %fusion = (f32[1,8,576]{2,1,0:T(8,128)}, f32[1,8,576]{2,1,0:T(8,128)}) fusion(f32[2,8,576]{2,1,0:T(8,128)} %shard_map.104), kind=kLoop, calls=%fused_computation | loop fusion | bytes 73728 | tf_op jit(solution)/shard_map/slice | solution.py:520

commit v6 on v5

--- a/solution.py
+++ b/solution.py
@@ -12,7 +12,7 @@
 CAMS = 64
 LANES = 128
 SCALE = 0.125
-TOG = 12
+TOG = 16
 MESH = pl.DeviceIdType.MESH
 F32 = jnp.float32
 BF16 = jnp.bfloat16
@@ -85,6 +85,8 @@
 
     tail = []
 
+    pl.semaphore_wait(barrier, len(offsets) + (n_cam - 1) + (n_pts - 1))
+
     def send(src, dst, ssem, rsem, device):
         copy = pltpu.make_async_remote_copy(
             src_ref=src, dst_ref=dst, send_sem=ssem, recv_sem=rsem, device_id=device, device_id_type=MESH
@@ -172,6 +174,10 @@
     rhs = packed(rhs_ref[0])
     damp = packed(damp_ref[0])
     precond = packed(precond_ref[0])
+    vecs[0] = rhs
+    scaled = precond * rhs
+    bases[0] = scaled
+    copies = start_gather(0, scaled)
     shift = (d // 2) * (2 * ct)
     spot = lax.broadcasted_iota(jnp.int32, (slots, width), 1)
     spot = jnp.where(spot < rows, spot, spot - rows)
@@ -191,11 +197,6 @@
         hot = jnp.transpose(hot)[:rows].astype(BF16)
         sum_hot[:, pl.ds(i * LANES, LANES)] = hot
         sum_hot[:, pl.ds(pairs + i * LANES, LANES)] = hot
-    pl.semaphore_wait(barrier, len(offsets) + (n_cam - 1) + (n_pts - 1))
-    vecs[0] = rhs
-    scaled = precond * rhs
-    bases[0] = scaled
-    copies = start_gather(0, scaled)
 
     loads[0].wait()
     loads[1].wait()

time: 126 us -> 122 us (0.968)
  Pallas kernels: 123 us -> 120 us
    pallas_call x1, Pallas kernels: 123 us -> 120 us  [on_device(): pl.pallas_call(functools.partial(kernel, n_pts, n_cam, tiles, slots, ct),...]
where the time goes in v6:
time: 122 us
  Pallas kernels  120 us (98%)
  local copies, waits for them, and re-layouts  1.36 us (1%)
    pallas_call x1, Pallas kernels, on_device(): pl.pallas_call(functools.partial(kernel, n_pts, n_cam, tiles, slots, ct),...  120 us

profile of v6, /device:TPU:1, one launch (start us, length us, event | category | flops | bytes accessed | tf_op | source)
XLA Modules:
  0.0 122.2 jit_solution(6237091570282610543)
XLA Ops:
  0.6 120.2 %shard_map.104 = f32[2,8,576]{2,1,0:T(8,128)} custom-call(f32[1,8,576]{2,1,0:T(8,128)} %rhs_ref.1, f32[1,8,576]{2,1,0:T(8,128)} %damp_ref.1, f32[1,8,576]{2,1,0:T(8,128)} %precond_ref.1, s32[1,8,96]{2,1,0:T(8,128)} %bitcast.7, s32[1,96]{1,0:T(1,128)} %counts_ref.1, f32[1,96,18,8,128]{4,3,2,1,0:T(8,128)} %bitcast.4, f32[1,96,6,8,128]{4,3,2,1,0:T(8,128)} %bitcast.5, ...), custom_call_target="tpu_custom_call" | custom-call | tf_op jit(solution)/shard_map/pallas_call | solution.py:482
  120.8 1.4 %fusion = (f32[1,8,576]{2,1,0:T(8,128)}, f32[1,8,576]{2,1,0:T(8,128)}) fusion(f32[2,8,576]{2,1,0:T(8,128)} %shard_map.104), kind=kLoop, calls=%fused_computation | loop fusion | bytes 73728 | tf_op jit(solution)/shard_map/slice | solution.py:521

commit v7 on v6

--- a/solution.py
+++ b/solution.py
@@ -12,7 +12,7 @@
 CAMS = 64
 LANES = 128
 SCALE = 0.125
-TOG = 16
+TOG = 24
 MESH = pl.DeviceIdType.MESH
 F32 = jnp.float32
 BF16 = jnp.bfloat16
@@ -376,11 +376,11 @@
             win_split[pl.ds(rows, rows), cut] = lo
 
         def pick(i, carry):
-            here = pl.ds(pl.multiple_of(i * (pairs // 2), 16), pairs // 2)
+            here = pl.ds(pl.multiple_of(i * pairs, 16), pairs)
             picked[here, :] = mm(pick_hot[here, pl.ds(0, 2 * rows)], win_split[...], NN)
             return carry
 
-        lax.fori_loop(0, 2, pick, 0)
+        lax.fori_loop(0, 1, pick, 0)
         look_step(0)
         bend = lax.fori_loop(0, steps, all_steps, jnp.zeros((slots, LANES), F32))
         sum_step(steps)

time: 122 us -> 122 us (level)
  no operation moved by 1% of the time
where the time goes in v7:
time: 122 us
  Pallas kernels  120 us (98%)
  local copies, waits for them, and re-layouts  1.36 us (1%)
    pallas_call x1, Pallas kernels, on_device(): pl.pallas_call(functools.partial(kernel, n_pts, n_cam, tiles, slots, ct),...  120 us

profile of v7, /device:TPU:1, one launch (start us, length us, event | category | flops | bytes accessed | tf_op | source)
XLA Modules:
  0.0 121.7 jit_solution(6940839853178200919)
XLA Ops:
  0.6 119.7 %shard_map.104 = f32[2,8,576]{2,1,0:T(8,128)} custom-call(f32[1,8,576]{2,1,0:T(8,128)} %rhs_ref.1, f32[1,8,576]{2,1,0:T(8,128)} %damp_ref.1, f32[1,8,576]{2,1,0:T(8,128)} %precond_ref.1, s32[1,8,96]{2,1,0:T(8,128)} %bitcast.7, s32[1,96]{1,0:T(1,128)} %counts_ref.1, f32[1,96,18,8,128]{4,3,2,1,0:T(8,128)} %bitcast.4, f32[1,96,6,8,128]{4,3,2,1,0:T(8,128)} %bitcast.5, ...), custom_call_target="tpu_custom_call" | custom-call | tf_op jit(solution)/shard_map/pallas_call | solution.py:482
  120.4 1.4 %fusion = (f32[1,8,576]{2,1,0:T(8,128)}, f32[1,8,576]{2,1,0:T(8,128)}) fusion(f32[2,8,576]{2,1,0:T(8,128)} %shard_map.104), kind=kLoop, calls=%fused_computation | loop fusion | bytes 73728 | tf_op jit(solution)/shard_map/slice | solution.py:521
